TPU v7x, 32 devices: a whole 2x2x4 slice. The times are simulated.
32 devices in a mesh: groups: 2 (over x), paths: 16 (over z, y, core).
Axes of the slice: x: 2, y: 2, z: 4, core: 2. Of those that a mesh axis runs over, the one named last changes fastest.
Arguments:
- path_basis: bfloat16 [4096, 512], P(('groups', 'paths')), parts along dimension 0, may hold values from -6 to 6
- proxy_weight: bfloat16 [4096, 512], P(('groups', 'paths')), parts along dimension 0, may hold values from -0.25 to 0.25
- notional: bfloat16 [4096], P(('groups', 'paths')), parts along dimension 0, may hold values from -4 to 4
- set_of: int32 [4096], P('groups'), parts along dimension 0, may hold values from 0 to 511
- threshold_index: int32 [1024], P('groups'), parts along dimension 0, may hold values from 0 to 15
- threshold_levels: float32 [32], P('groups'), parts along dimension 0, may hold values from 0.5 to 20
- loss_rate: float32 [1024], P('groups'), parts along dimension 0, may hold values from 0.4 to 1
Outputs:
- expected_loss: float32 [2], P('groups'), parts along dimension 0
- basis_adjoint: float32 [4096, 512], P(('groups', 'paths')), parts along dimension 0
- weight_adjoint: float32 [4096, 512], P(('groups', 'paths')), parts along dimension 0
There are 2 independent parts, one for each index of `groups`. A program takes and returns all parts, laid end to end along the dimension named above; each array names one. Nothing has to cross between parts.
Inputs may be any that keep to these rules, and one draw needn't show every extreme that they name: `set_of`: netting set of each trade; set sizes are uneven.
All inputs are finite; a program needn't handle non-finite values.
Results may differ from a plain program's by a relative error of at most 0.0041.
Values may be sent and summed in bfloat16 or wider, within the bound.
A program may use at most 64 MiB of HBM per device.

v0:
```python
import functools
import math

import jax
import jax.numpy as jnp
from jax import lax
from jax.experimental import pallas as pl
from jax.experimental.pallas import tpu as pltpu
from jax.sharding import PartitionSpec as P

REGRESSORS = 32
RIDGE_SCALE = 0.01
PRECISE = lax.Precision.HIGHEST
LANES = 128
PIECES = 4
F32 = jnp.float32
BF16 = jnp.bfloat16

NN = (((1,), (0,)), ((), ()))
NT = (((1,), (1,)), ((), ()))
TN = (((0,), (0,)), ((), ()))


def mm(a, b, dims=NN):
    return lax.dot_general(a, b, dims, preferred_element_type=F32)


def precise(a, b, dims=NN):
    return lax.dot_general(a, b, dims, precision=PRECISE, preferred_element_type=F32)


def split3(x):
    hi = x.astype(BF16)
    rest = x - hi.astype(F32)
    mid = rest.astype(BF16)
    lo = (rest - mid.astype(F32)).astype(BF16)
    return hi, mid, lo


def stack3(x):
    hi, mid, lo = split3(x)
    return jnp.concatenate([hi, mid, lo, jnp.zeros_like(hi)], axis=0)


def design_of(basis):
    front = pltpu.roll(basis[:, :LANES].astype(F32), 1, 1)
    lane = lax.broadcasted_iota(jnp.int32, front.shape, 1)
    return jnp.where(lane == 0, 1.0, jnp.where(lane < REGRESSORS, front, 0.0))


def triple(design):
    return (
        design + pltpu.roll(design, REGRESSORS, 1) + pltpu.roll(design, 2 * REGRESSORS, 1)
    ).astype(BF16)


def spd_inverse(gram, between):
    size = REGRESSORS
    row = lax.broadcasted_iota(jnp.int32, (size, LANES), 0)
    lane = lax.broadcasted_iota(jnp.int32, (size, LANES), 1)
    work = jnp.where(lane < size, gram, jnp.where(lane == row + size, 1.0, 0.0))
    for k in range(size):
        if k == size // 3:
            between()
        column = jnp.broadcast_to(work[:, k : k + 1], work.shape)
        pivot = work[k : k + 1, :] / column[k : k + 1, :]
        work = jnp.where(row == k, pivot, work - column * pivot)
    return pltpu.roll(work, LANES - size, 1)


def set_table(labels, set_total):
    sets = lax.broadcasted_iota(jnp.int32, (set_total, labels.shape[1]), 0)
    return jnp.where(sets == labels, 1.0, 0.0).astype(BF16)


def partner(index, step, count):
    if count & (count - 1):
        return lax.rem(index + step, count)
    result, weight = 0, 1
    while weight < count:
        bit = lax.rem(lax.div(index, weight), 2)
        result = result + weight * (1 - bit if step & weight else bit)
        weight *= 2
    return result


def kernel(
    inner, outer, paths_all, set_total,
    pb_hbm, w_hbm, not_hbm, set_hbm, tidx_hbm, level_hbm, rate_hbm,
    loss_ref, basis_ref, wadj_ref,
    not_ref, set_ref, tidx_ref, level_ref, rate_ref,
    pall, wall, nall, nsend, gown, gall, gq, dstack, table, invert,
    bown, bq, bzsend, bz, csend, cq, ssend, sq,
    eown, eq, wown, wz, pown, pq, nsig, tval,
    via, local, zsend, zrecv, qsend, qrecv, steps,
):
    rows, feats = basis_ref.shape
    trades = wadj_ref.shape[0]
    quarter = set_total // inner
    me = lax.axis_index("paths")
    q = lax.rem(me, inner)
    z = lax.div(me, inner)

    loads = [
        pltpu.make_async_copy(source, target, local.at[i])
        for i, (source, target) in enumerate(
            [
                (pb_hbm, pall.at[q]),
                (not_hbm, not_ref),
                (w_hbm, wall.at[z]),
                (set_hbm, set_ref),
                (tidx_hbm, tidx_ref),
                (level_hbm, level_ref),
                (rate_hbm, rate_ref),
            ]
        )
    ]
    for load in loads:
        load.start()

    barrier = pltpu.get_barrier_semaphore()
    for d in range(1, inner):
        pl.semaphore_signal(
            barrier, inc=1, device_id={"paths": z * inner + lax.rem(q + d, inner)},
            device_id_type=pl.DeviceIdType.MESH,
        )
    for d in range(1, outer):
        pl.semaphore_signal(
            barrier, inc=1, device_id={"paths": lax.rem(z + d, outer) * inner + q},
            device_id_type=pl.DeviceIdType.MESH,
        )

    pending = []

    def over_q(which, source, target):
        copies = []
        for d in range(inner - 1, 0, -1):
            peer = partner(q, d, inner)
            copy = pltpu.make_async_remote_copy(
                src_ref=source(peer), dst_ref=target.at[q],
                send_sem=qsend.at[which, d - 1], recv_sem=qrecv.at[which, d - 1],
                device_id={"paths": z * inner + peer},
                device_id_type=pl.DeviceIdType.MESH,
            )
            copy.start()
            copies.append(copy)
        pending.extend(copies)
        return copies

    def over_z(which, source, target):
        copies = []
        for d in range(outer - 1, 0, -1):
            peer = partner(z, d, outer)
            copy = pltpu.make_async_remote_copy(
                src_ref=source(peer), dst_ref=target.at[z],
                send_sem=zsend.at[which, d - 1], recv_sem=zrecv.at[which, d - 1],
                device_id={"paths": peer * inner + q},
                device_id_type=pl.DeviceIdType.MESH,
            )
            copy.start()
            copies.append(copy)
        pending.extend(copies)
        return copies

    def arrive(copies):
        for copy in copies:
            copy.wait_recv()

    relay = outer == 4 and trades % (16 * PIECES) == 0
    part = trades // PIECES
    edge = z * (3 - z) == 0
    near, far, mid = partner(z, 1, outer), partner(z, 2, outer), partner(z, 3, outer)

    def piece(source, target, p, row, peer):
        cut = pl.ds(p * part, part)
        return pltpu.make_async_remote_copy(
            src_ref=source.at[cut], dst_ref=target.at[cut],
            send_sem=steps.at[row, p], recv_sem=steps.at[row + 1, p],
            device_id={"paths": peer * inner + q}, device_id_type=pl.DeviceIdType.MESH,
        )

    def block(source, target, which, lane, peer):
        return pltpu.make_async_remote_copy(
            src_ref=source, dst_ref=target,
            send_sem=zsend.at[which, lane], recv_sem=zrecv.at[which, lane],
            device_id={"paths": peer * inner + q}, device_id_type=pl.DeviceIdType.MESH,
        )

    def total(ref, count):
        result = ref[0].astype(F32)
        for i in range(1, count):
            result = result + ref[i].astype(F32)
        return result

    loads[0].wait()
    own_design = design_of(pall[q])
    own_triple = triple(own_design)
    own_turned = jnp.transpose(own_design)[:REGRESSORS, :].astype(BF16)
    gown[...] = own_turned
    loads[1].wait()
    nrow = jnp.broadcast_to(not_ref[...].astype(F32), (8, trades))
    nsend[...] = nrow
    loads[2].wait()
    pl.semaphore_wait(barrier, inner + outer - 2)

    gram_z = over_z(0, lambda peer: gown, gall)
    note_z = over_z(1, lambda peer: nsend, nall)
    if relay:
        far_in = [piece(wall.at[z], wall.at[z], p, 0, far) for p in range(PIECES)]
        near_in = block(wall.at[z], wall.at[z], 2, 0, near)
        mid_in = block(wall.at[z], wall.at[z], 2, 1, mid)
        handed = [piece(wall.at[far], wall.at[far], p, 2, near) for p in range(PIECES)]
        for copy in far_in:
            copy.start()
        near_in.start()
        pending.extend(far_in + [near_in])

        @pl.when(jnp.logical_not(edge))
        def _():
            mid_in.start()
    else:
        trade_z = over_z(2, lambda peer: wall.at[z], wall)

    def forward(p):
        if relay:
            far_in[p].wait_recv()

            @pl.when(jnp.logical_not(edge))
            def _():
                handed[p].start()

    path_q = over_q(0, lambda peer: pall.at[q], pall)
    gall[z] = own_turned
    nall[z] = nrow

    arrive(gram_z)
    gram_q = over_q(1, lambda peer: gall, gq)
    gq[q] = gall[...]

    for load in loads[3:]:
        load.wait()
    all_levels = tidx_ref[...]
    all_thresholds = jnp.zeros((inner, quarter), F32)
    levels = tidx_ref[pl.ds(q, 1), :]
    thresholds = jnp.zeros((1, quarter), F32)
    for i in range(level_ref.shape[0]):
        thresholds = jnp.where(levels == i, level_ref[i], thresholds)
        all_thresholds = jnp.where(all_levels == i, level_ref[i], all_thresholds)
    thresholds = jnp.transpose(jnp.broadcast_to(thresholds, (quarter, quarter)))[:, :1]
    rate = jnp.transpose(
        jnp.broadcast_to(rate_ref[pl.ds(q, 1), :], (quarter, quarter))
    )[:, :1]
    all_rates = rate_ref[...]
    labels = jnp.concatenate(
        [set_ref[pl.ds(i * inner + q, 1), :] for i in range(outer)], axis=1
    )
    table[...] = set_table(labels, set_total)

    forward(0)
    arrive(path_q)
    paths = pall[...].reshape(inner * rows, feats)
    design = design_of(paths)
    design3 = triple(design)
    design_t = jnp.transpose(design)[:REGRESSORS, :].astype(BF16)

    forward(1)
    arrive(gram_q)
    turned_all = jnp.concatenate(
        [gq[i, j] for i in range(inner) for j in range(outer)], axis=1
    )
    dstack[...] = jnp.concatenate(
        [turned_all, turned_all, turned_all, jnp.zeros_like(turned_all)], axis=0
    )
    gram = mm(turned_all, dstack[...], NT)
    forward(2)
    gram_row = lax.broadcasted_iota(jnp.int32, (REGRESSORS, LANES), 0)
    gram_lane = lax.broadcasted_iota(jnp.int32, (REGRESSORS, LANES), 1)
    ridge = jnp.where(gram_row == gram_lane, RIDGE_SCALE * paths_all, 0.0)
    invert[...] = spd_inverse(gram + ridge, lambda: forward(3))

    arrive(note_z)
    notional = jnp.concatenate([nall[i][0:1, :] for i in range(outer)], axis=1)
    if relay:
        near_in.wait_recv()

        @pl.when(jnp.logical_not(edge))
        def _():
            mid_in.wait_recv()

        @pl.when(edge)
        def _():
            for copy in handed:
                copy.wait_recv()
    else:
        arrive(trade_z)
    weights = wall[...].reshape(outer * trades, feats)
    pre_act = mm(paths, weights, NT)
    small = jnp.exp(-jnp.abs(pre_act))
    tval[...] = (notional * (jnp.maximum(pre_act, 0.0) + jnp.log1p(small))).astype(BF16)
    nsig[...] = notional * (jnp.where(pre_act >= 0.0, 1.0, small) / (1.0 + small))

    by_trade = mm(design_t, tval[...])
    by_set = mm(jnp.concatenate(split3(by_trade), axis=0), table[...], NT)
    moments = (
        by_set[:REGRESSORS] + by_set[REGRESSORS : 2 * REGRESSORS] + by_set[2 * REGRESSORS :]
    )
    for i in range(inner):
        bown[i] = moments[:, i * quarter : (i + 1) * quarter]
    moment_q = over_q(2, lambda peer: bown.at[peer], bq)
    bq[q] = bown[q]
    arrive(moment_q)
    moment_mid = total(bq, inner)
    bzsend[...] = moment_mid
    moment_z = over_z(3, lambda peer: bzsend, bz)
    bz[z] = moment_mid
    arrive(moment_z)
    inverse = invert[:, :REGRESSORS]
    coeffs = precise(inverse, total(bz, outer))
    csend[...] = coeffs
    coeffs_q = over_q(3, lambda peer: csend, cq)
    cq[q] = coeffs
    excess = mm(stack3(coeffs), dstack[...], TN) - thresholds
    fade = jnp.exp(-jnp.abs(excess))
    loss = jnp.maximum(excess, 0.0) + jnp.log1p(fade)
    seed = rate * (jnp.where(excess >= 0.0, 1.0, fade) / (1.0 + fade))
    seed_cut = mm(dstack[:REGRESSORS, :], jnp.concatenate(split3(seed), axis=0), NT)
    seed_sum = (
        seed_cut[:, :quarter] + seed_cut[:, quarter : 2 * quarter] + seed_cut[:, 2 * quarter :]
    )
    solved = precise(inverse, seed_sum)
    loss_part = jnp.sum(rate * jnp.sum(loss, axis=1, keepdims=True), axis=0, keepdims=True)
    answer = jnp.concatenate([solved, jnp.broadcast_to(loss_part, (8, quarter))], axis=0)
    ssend[...] = answer
    answer_q = over_q(4, lambda peer: ssend, sq)
    sq[q] = answer
    arrive(coeffs_q)
    coeffs_all = jnp.concatenate([cq[i] for i in range(inner)], axis=1)
    arrive(answer_q)
    answers = jnp.concatenate([sq[i] for i in range(inner)], axis=1)
    solved_all = answers[:REGRESSORS]
    loss_sum = jnp.sum(answers[REGRESSORS : REGRESSORS + 1], axis=1, keepdims=True) / quarter
    loss_ref[...] = jnp.broadcast_to(loss_sum / (paths_all * set_total), loss_ref.shape)

    picked = mm(jnp.concatenate(split3(solved_all), axis=0), table[...])
    solved3 = jnp.concatenate(
        [picked.astype(BF16), jnp.zeros((LANES - 3 * REGRESSORS, picked.shape[1]), BF16)], axis=0
    )
    spread = mm(design3, solved3).astype(BF16).astype(F32)
    slopes = (nsig[...] * spread).astype(BF16)
    scale = 1.0 / math.sqrt(paths_all)
    weight_part = mm(slopes, paths, TN) * scale
    wown[...] = weight_part.astype(BF16).reshape(outer, trades, feats)
    if relay:
        carried = [piece(wown.at[mid], via, p, 6, near) for p in range(PIECES)]
        far_out = [piece(wown.at[far], wz.at[z], p, 4, far) for p in range(PIECES)]
        near_out = block(wown.at[near], wz.at[z], 4, 0, near)
        mid_out = block(wown.at[mid], wz.at[z], 4, 1, mid)

        @pl.when(edge)
        def _():
            for copy in carried:
                copy.start()
            for copy in far_out:
                copy.start()
            wz[mid] = jnp.zeros_like(via)

        @pl.when(jnp.logical_not(edge))
        def _():
            mid_out.start()

        near_out.start()
        pending.extend(far_out + [near_out])
    else:
        weight_z = over_z(4, lambda peer: wown.at[peer], wz)
    wz[z] = wown[z]

    pulled = mm(solved3, tval[...], NT)
    pulled = (
        pulled[:REGRESSORS]
        + pulled[REGRESSORS : 2 * REGRESSORS]
        + pulled[2 * REGRESSORS : 3 * REGRESSORS]
    )
    for i in range(inner):
        eown[i] = pulled[:, i * rows : (i + 1) * rows]
    pull_q = over_q(5, lambda peer: eown.at[peer], eq)
    eq[q] = eown[q]
    basis_part = mm(slopes, weights)
    pown[...] = basis_part.astype(BF16).reshape(inner, rows, feats)
    basis_q = over_q(6, lambda peer: pown.at[peer], pq)
    pq[q] = pown[q]

    if relay:

        @pl.when(jnp.logical_not(edge))
        def _():
            for p in range(PIECES):
                carried[p].wait_recv()
                cut = pl.ds(p * part, part)
                joint = wown[far, cut, :].astype(F32) + via[cut, :].astype(F32)
                wown[far, cut, :] = joint.astype(BF16)
                far_out[p].start()

    fitted = mm(own_triple, stack3(coeffs_all))
    full_thresholds = jnp.concatenate([all_thresholds[i : i + 1] for i in range(inner)], axis=1)
    full_rates = jnp.concatenate([all_rates[i : i + 1] for i in range(inner)], axis=1)
    over = fitted - full_thresholds
    tail = jnp.exp(-jnp.abs(over))
    own_seed = full_rates * (jnp.where(over >= 0.0, 1.0, tail) / (1.0 + tail))
    residual = own_seed - mm(own_triple, stack3(solved_all))
    term = precise(coeffs_all, residual, NT) - precise(solved_all, fitted, NT)
    arrive(pull_q)
    term = term + total(eq, inner)
    padded = jnp.concatenate([term, jnp.zeros((LANES - REGRESSORS, rows), F32)], axis=0)
    turned = pltpu.roll(jnp.transpose(padded), LANES - 1, 1)
    lane = lax.broadcasted_iota(jnp.int32, turned.shape, 1)
    turned = jnp.where(lane < REGRESSORS - 1, turned, 0.0)
    arrive(basis_q)
    basis_ref[...] = total(pq, inner)
    basis_ref[:, :LANES] = basis_ref[:, :LANES] + turned
    if relay:
        arrive(far_out)
        near_out.wait_recv()

        @pl.when(jnp.logical_not(edge))
        def _():
            mid_out.wait_recv()
            mid_out.wait_send()
            mid_in.wait_send()
            for copy in handed:
                copy.wait_send()

        @pl.when(edge)
        def _():
            for copy in carried:
                copy.wait_send()
    else:
        arrive(weight_z)
    wadj_ref[...] = total(wz, outer)
    for copy in pending:
        copy.wait_send()


def shards(
    path_basis, proxy_weight, notional, set_of, threshold_index, threshold_levels, loss_rate
):
    count = lax.axis_size("paths")
    inner = math.gcd(4, count)
    outer = count // inner
    rows, feats = path_basis.shape
    trades = proxy_weight.shape[0]
    set_total = loss_rate.shape[0]
    quarter = set_total // inner
    size = REGRESSORS
    vmem = pl.BlockSpec(memory_space=pltpu.VMEM)
    z_pairs, q_pairs = max(outer - 1, 1), max(inner - 1, 1)
    loss, basis_adjoint, weight_adjoint = pl.pallas_call(
        functools.partial(kernel, inner, outer, rows * count, set_total),
        out_shape=(
            jax.ShapeDtypeStruct((1, LANES), F32),
            jax.ShapeDtypeStruct((rows, feats), F32),
            jax.ShapeDtypeStruct((trades, feats), F32),
        ),
        in_specs=[pl.BlockSpec(memory_space=pltpu.HBM)] * 7,
        out_specs=(vmem, vmem, vmem),
        scratch_shapes=[
            pltpu.VMEM((1, trades), BF16),
            pltpu.VMEM((inner * outer, trades), jnp.int32),
            pltpu.VMEM((inner, quarter), jnp.int32),
            pltpu.SMEM(threshold_levels.shape, F32),
            pltpu.VMEM((inner, quarter), F32),
            pltpu.VMEM((inner, rows, feats), BF16),
            pltpu.VMEM((outer, trades, feats), BF16),
            pltpu.VMEM((outer, 8, trades), F32),
            pltpu.VMEM((8, trades), F32),
            pltpu.VMEM((size, rows), BF16),
            pltpu.VMEM((outer, size, rows), BF16),
            pltpu.VMEM((inner, outer, size, rows), BF16),
            pltpu.VMEM((LANES, count * rows), BF16),
            pltpu.VMEM((set_total, outer * trades), BF16),
            pltpu.VMEM((size, LANES), F32),
            pltpu.VMEM((inner, size, quarter), F32),
            pltpu.VMEM((inner, size, quarter), F32),
            pltpu.VMEM((size, quarter), F32),
            pltpu.VMEM((outer, size, quarter), F32),
            pltpu.VMEM((size, quarter), F32),
            pltpu.VMEM((inner, size, quarter), F32),
            pltpu.VMEM((size + 8, quarter), F32),
            pltpu.VMEM((inner, size + 8, quarter), F32),
            pltpu.VMEM((inner, size, rows), F32),
            pltpu.VMEM((inner, size, rows), F32),
            pltpu.VMEM((outer, trades, feats), BF16),
            pltpu.VMEM((outer, trades, feats), BF16),
            pltpu.VMEM((inner, rows, feats), BF16),
            pltpu.VMEM((inner, rows, feats), BF16),
            pltpu.VMEM((inner * rows, outer * trades), F32),
            pltpu.VMEM((inner * rows, outer * trades), BF16),
            pltpu.VMEM((trades, feats), BF16),
            pltpu.SemaphoreType.DMA((7,)),
            pltpu.SemaphoreType.DMA((5, z_pairs)),
            pltpu.SemaphoreType.DMA((5, z_pairs)),
            pltpu.SemaphoreType.DMA((7, q_pairs)),
            pltpu.SemaphoreType.DMA((7, q_pairs)),
            pltpu.SemaphoreType.DMA((8, PIECES)),
        ],
        compiler_params=pltpu.CompilerParams(
            collective_id=0, has_side_effects=True, vmem_limit_bytes=48 * 1024 * 1024
        ),
    )(
        *(
            pltpu.with_memory_space_constraint(operand, pltpu.HBM)
            for operand in (
                path_basis,
                proxy_weight,
                notional.reshape(1, trades),
                set_of.reshape(-1, trades),
                threshold_index.reshape(inner, quarter),
                threshold_levels,
                loss_rate.reshape(inner, quarter),
            )
        )
    )
    return loss[0, :1], basis_adjoint, weight_adjoint


def solution(mesh):
    placed = (
        P(("groups", "paths"), None),
        P(("groups", "paths"), None),
        P(("groups", "paths")),
        P("groups"),
        P("groups"),
        P("groups"),
        P("groups"),
    )
    return jax.shard_map(
        shards,
        mesh=mesh,
        in_specs=placed,
        out_specs=(P("groups"), P(("groups", "paths"), None), P(("groups", "paths"), None)),
        check_vma=False,
    )
```

profile of v0, /device:TPU:0, one launch (start us, length us, event | category | flops | bytes accessed | tf_op | source)
XLA Modules:
  0.0 45.8 jit_solution(16725234106217560142)
XLA Ops:
  0.6 42.6 %shard_map.94 = (f32[1,128]{1,0:T(1,128)S(1)}, f32[128,512]{1,0:T(8,128)S(1)}, f32[128,512]{1,0:T(8,128)S(1)}) custom-call(bf16[128,512]{1,0:T(8,128)(2,1)} %pb_hbm.1, bf16[128,512]{1,0:T(8,128)(2,1)} %w_hbm.1, bf16[1,128]{1,0:T(2,128)(2,1)} %bitcast.10, s32[16,128]{1,0:T(8,128)} %bitcast.7, s32[4,128]{1,0:T(4,128)} %bitcast.8, f32[16]{0:T(128)} %level_hbm.1, ...), custom_call_target="tpu_custom_call" | custom-call | tf_op jit(solution)/shard_map/pallas_call | solution.py:456
  43.2 0.7 %copy.14 = f32[128,512]{1,0:T(8,128)} copy(f32[128,512]{1,0:T(8,128)S(1)} %get-tuple-element.13) | data formatting | bytes 524288
  44.0 0.7 %copy.15 = f32[128,512]{1,0:T(8,128)} copy(f32[128,512]{1,0:T(8,128)S(1)} %get-tuple-element.14) | data formatting | bytes 524288
where the time goes:
time: 45.9 us; the launch traced here: 45.8 us
  Pallas kernels  42.6 us (93%)
  between operations  1.8 us (4%)
  local copies, waits for them, and re-layouts  1.41 us (3%)
    pallas_call x1, Pallas kernels, shards(): pl.pallas_call(functools.partial(kernel, inner, outer, rows * count, set_...  42.6 us
    unnamed x2, local copies, waits for them, and re-layouts  1.41 us

commit v1 on v0

--- a/solution.py
+++ b/solution.py
@@ -13,6 +13,8 @@
 PRECISE = lax.Precision.HIGHEST
 LANES = 128
 PIECES = 4
+FIRST_STEPS = 12
+COPIES = 64
 F32 = jnp.float32
 BF16 = jnp.bfloat16
 
@@ -54,18 +56,24 @@
     ).astype(BF16)
 
 
-def spd_inverse(gram, between):
-    size = REGRESSORS
-    row = lax.broadcasted_iota(jnp.int32, (size, LANES), 0)
-    lane = lax.broadcasted_iota(jnp.int32, (size, LANES), 1)
-    work = jnp.where(lane < size, gram, jnp.where(lane == row + size, 1.0, 0.0))
-    for k in range(size):
-        if k == size // 3:
-            between()
+def augmented(gram):
+    row = lax.broadcasted_iota(jnp.int32, gram.shape, 0)
+    lane = lax.broadcasted_iota(jnp.int32, gram.shape, 1)
+    return jnp.where(lane < REGRESSORS, gram, jnp.where(lane == row + REGRESSORS, 1.0, 0.0))
+
+
+def eliminate(work, first, last):
+    row = lax.broadcasted_iota(jnp.int32, work.shape, 0)
+    for k in range(first, last):
         column = jnp.broadcast_to(work[:, k : k + 1], work.shape)
         pivot = work[k : k + 1, :] / column[k : k + 1, :]
         work = jnp.where(row == k, pivot, work - column * pivot)
-    return pltpu.roll(work, LANES - size, 1)
+    return work
+
+
+def spd_inverse(gram):
+    work = eliminate(augmented(gram), 0, REGRESSORS)
+    return pltpu.roll(work, LANES - REGRESSORS, 1)
 
 
 def set_table(labels, set_total):
@@ -92,7 +100,7 @@
     pall, wall, nall, nsend, gown, gall, gq, dstack, table, invert,
     bown, bq, bzsend, bz, csend, cq, ssend, sq,
     eown, eq, wown, wz, pown, pq, nsig, tval,
-    via, local, zsend, zrecv, qsend, qrecv, steps,
+    local, zsend, zrecv, qsend, qrecv,
 ):
     rows, feats = basis_ref.shape
     trades = wadj_ref.shape[0]
@@ -166,26 +174,6 @@
         for copy in copies:
             copy.wait_recv()
 
-    relay = outer == 4 and trades % (16 * PIECES) == 0
-    part = trades // PIECES
-    edge = z * (3 - z) == 0
-    near, far, mid = partner(z, 1, outer), partner(z, 2, outer), partner(z, 3, outer)
-
-    def piece(source, target, p, row, peer):
-        cut = pl.ds(p * part, part)
-        return pltpu.make_async_remote_copy(
-            src_ref=source.at[cut], dst_ref=target.at[cut],
-            send_sem=steps.at[row, p], recv_sem=steps.at[row + 1, p],
-            device_id={"paths": peer * inner + q}, device_id_type=pl.DeviceIdType.MESH,
-        )
-
-    def block(source, target, which, lane, peer):
-        return pltpu.make_async_remote_copy(
-            src_ref=source, dst_ref=target,
-            send_sem=zsend.at[which, lane], recv_sem=zrecv.at[which, lane],
-            device_id={"paths": peer * inner + q}, device_id_type=pl.DeviceIdType.MESH,
-        )
-
     def total(ref, count):
         result = ref[0].astype(F32)
         for i in range(1, count):
@@ -205,30 +193,7 @@
 
     gram_z = over_z(0, lambda peer: gown, gall)
     note_z = over_z(1, lambda peer: nsend, nall)
-    if relay:
-        far_in = [piece(wall.at[z], wall.at[z], p, 0, far) for p in range(PIECES)]
-        near_in = block(wall.at[z], wall.at[z], 2, 0, near)
-        mid_in = block(wall.at[z], wall.at[z], 2, 1, mid)
-        handed = [piece(wall.at[far], wall.at[far], p, 2, near) for p in range(PIECES)]
-        for copy in far_in:
-            copy.start()
-        near_in.start()
-        pending.extend(far_in + [near_in])
-
-        @pl.when(jnp.logical_not(edge))
-        def _():
-            mid_in.start()
-    else:
-        trade_z = over_z(2, lambda peer: wall.at[z], wall)
-
-    def forward(p):
-        if relay:
-            far_in[p].wait_recv()
-
-            @pl.when(jnp.logical_not(edge))
-            def _():
-                handed[p].start()
-
+    trade_z = over_z(2, lambda peer: wall.at[z], wall)
     path_q = over_q(0, lambda peer: pall.at[q], pall)
     gall[z] = own_turned
     nall[z] = nrow
@@ -256,14 +221,12 @@
     )
     table[...] = set_table(labels, set_total)
 
-    forward(0)
     arrive(path_q)
     paths = pall[...].reshape(inner * rows, feats)
     design = design_of(paths)
     design3 = triple(design)
     design_t = jnp.transpose(design)[:REGRESSORS, :].astype(BF16)
 
-    forward(1)
     arrive(gram_q)
     turned_all = jnp.concatenate(
         [gq[i, j] for i in range(inner) for j in range(outer)], axis=1
@@ -272,27 +235,14 @@
         [turned_all, turned_all, turned_all, jnp.zeros_like(turned_all)], axis=0
     )
     gram = mm(turned_all, dstack[...], NT)
-    forward(2)
     gram_row = lax.broadcasted_iota(jnp.int32, (REGRESSORS, LANES), 0)
     gram_lane = lax.broadcasted_iota(jnp.int32, (REGRESSORS, LANES), 1)
     ridge = jnp.where(gram_row == gram_lane, RIDGE_SCALE * paths_all, 0.0)
-    invert[...] = spd_inverse(gram + ridge, lambda: forward(3))
+    invert[...] = spd_inverse(gram + ridge)
 
     arrive(note_z)
     notional = jnp.concatenate([nall[i][0:1, :] for i in range(outer)], axis=1)
-    if relay:
-        near_in.wait_recv()
-
-        @pl.when(jnp.logical_not(edge))
-        def _():
-            mid_in.wait_recv()
-
-        @pl.when(edge)
-        def _():
-            for copy in handed:
-                copy.wait_recv()
-    else:
-        arrive(trade_z)
+    arrive(trade_z)
     weights = wall[...].reshape(outer * trades, feats)
     pre_act = mm(paths, weights, NT)
     small = jnp.exp(-jnp.abs(pre_act))
@@ -350,28 +300,7 @@
     scale = 1.0 / math.sqrt(paths_all)
     weight_part = mm(slopes, paths, TN) * scale
     wown[...] = weight_part.astype(BF16).reshape(outer, trades, feats)
-    if relay:
-        carried = [piece(wown.at[mid], via, p, 6, near) for p in range(PIECES)]
-        far_out = [piece(wown.at[far], wz.at[z], p, 4, far) for p in range(PIECES)]
-        near_out = block(wown.at[near], wz.at[z], 4, 0, near)
-        mid_out = block(wown.at[mid], wz.at[z], 4, 1, mid)
-
-        @pl.when(edge)
-        def _():
-            for copy in carried:
-                copy.start()
-            for copy in far_out:
-                copy.start()
-            wz[mid] = jnp.zeros_like(via)
-
-        @pl.when(jnp.logical_not(edge))
-        def _():
-            mid_out.start()
-
-        near_out.start()
-        pending.extend(far_out + [near_out])
-    else:
-        weight_z = over_z(4, lambda peer: wown.at[peer], wz)
+    weight_z = over_z(4, lambda peer: wown.at[peer], wz)
     wz[z] = wown[z]
 
     pulled = mm(solved3, tval[...], NT)
@@ -388,17 +317,6 @@
     pown[...] = basis_part.astype(BF16).reshape(inner, rows, feats)
     basis_q = over_q(6, lambda peer: pown.at[peer], pq)
     pq[q] = pown[q]
-
-    if relay:
-
-        @pl.when(jnp.logical_not(edge))
-        def _():
-            for p in range(PIECES):
-                carried[p].wait_recv()
-                cut = pl.ds(p * part, part)
-                joint = wown[far, cut, :].astype(F32) + via[cut, :].astype(F32)
-                wown[far, cut, :] = joint.astype(BF16)
-                far_out[p].start()
 
     fitted = mm(own_triple, stack3(coeffs_all))
     full_thresholds = jnp.concatenate([all_thresholds[i : i + 1] for i in range(inner)], axis=1)
@@ -417,27 +335,422 @@
     arrive(basis_q)
     basis_ref[...] = total(pq, inner)
     basis_ref[:, :LANES] = basis_ref[:, :LANES] + turned
-    if relay:
-        arrive(far_out)
-        near_out.wait_recv()
-
-        @pl.when(jnp.logical_not(edge))
-        def _():
-            mid_out.wait_recv()
-            mid_out.wait_send()
-            mid_in.wait_send()
-            for copy in handed:
-                copy.wait_send()
-
-        @pl.when(edge)
-        def _():
-            for copy in carried:
-                copy.wait_send()
-    else:
-        arrive(weight_z)
+    arrive(weight_z)
     wadj_ref[...] = total(wz, outer)
     for copy in pending:
         copy.wait_send()
+
+
+def square(
+    paths_all, set_total,
+    pb_hbm, w_hbm, not_hbm, set_hbm, tidx_hbm, level_hbm, rate_hbm,
+    loss_ref, basis_ref, wadj_ref,
+    not_ref, set_ref, tidx_ref, level_ref, rate_ref,
+    pall, wall, small, dall, dgrid, dstack, dtri, dturn, table, invert,
+    bown, bq, bzsend, bz, csend, cq, ssend, sq, lsend, lq, over_ref,
+    tval, nsig, slopes,
+    wsend, wvia, wnear, wjoin, wz, psend, pvia, pfar, pjoin, pq, esend, evia, ejoin, eq,
+    local, send, recv,
+):
+    rows, feats = basis_ref.shape
+    trades = wadj_ref.shape[0]
+    quarter = set_total // 4
+    me = lax.axis_index("paths")
+    q, z = lax.rem(me, 4), lax.div(me, 4)
+    peers = [me] + [partner(me, step, 16) for step in range(1, 16)]
+    CORE, SIDE, NEAR, FAR = 1, 2, 4, 8
+    trade_steps = (0, NEAR, SIDE, NEAR + SIDE)
+    path_steps = (0, CORE, FAR, CORE + FAR)
+
+    loads = [
+        pltpu.make_async_copy(source, target, local.at[i])
+        for i, (source, target) in enumerate(
+            [
+                (pb_hbm, pall.at[0]),
+                (not_hbm, not_ref),
+                (w_hbm, wall.at[0]),
+                (set_hbm, set_ref),
+                (tidx_hbm, tidx_ref),
+                (level_hbm, level_ref),
+                (rate_hbm, rate_ref),
+            ]
+        )
+    ]
+    barrier = pltpu.get_barrier_semaphore()
+    for step in (CORE, SIDE, NEAR, FAR):
+        pl.semaphore_signal(
+            barrier, inc=1, device_id={"paths": peers[step]},
+            device_id_type=pl.DeviceIdType.MESH,
+        )
+    for load in loads:
+        load.start()
+
+    copies = []
+
+    def remote(source, target, step):
+        k = len(copies)
+        copy = pltpu.make_async_remote_copy(
+            src_ref=source, dst_ref=target, send_sem=send.at[k], recv_sem=recv.at[k],
+            device_id={"paths": peers[step]}, device_id_type=pl.DeviceIdType.MESH,
+        )
+        copies.append(copy)
+        return copy
+
+    def start(*group):
+        for copy in group:
+            copy.start()
+
+    def arrive(*group):
+        for copy in group:
+            copy.wait_recv()
+
+    def pieces(source, target, step, extent):
+        part = extent // PIECES
+        cuts = [pl.ds(p * part, part) for p in range(PIECES)]
+        return [remote(source.at[cut], target.at[cut], step) for cut in cuts]
+
+    def grouped(source, target, bits):
+        return [remote(source(peers[s]), target, s) for s in bits]
+
+    def place(i):
+        design = design_of(pall[i])
+        at = slice(i * rows, (i + 1) * rows)
+        dtri[at, :] = triple(design)
+        turned = jnp.transpose(design)[:REGRESSORS, :].astype(BF16)
+        dturn[:, at] = turned
+        return turned
+
+    loads[0].wait()
+    own_turned = place(0)
+    loads[1].wait()
+    note = jnp.broadcast_to(not_ref[...].astype(F32), (16, trades)).astype(BF16)
+    small[0] = jnp.concatenate([own_turned, note], axis=0)
+    loads[2].wait()
+    pl.semaphore_wait(barrier, 4)
+
+    small_near = remote(small.at[0], small.at[1], NEAR)
+    small_side = remote(small.at[0], small.at[2], SIDE)
+    trade_near = pieces(wall.at[0], wall.at[1], NEAR, trades)
+    path_core = remote(pall.at[0], pall.at[1], CORE)
+    trade_side = remote(wall.at[0], wall.at[2], SIDE)
+    path_far = pieces(pall.at[0], pall.at[2], FAR, rows)
+    start(small_near, small_side, *trade_near, path_core, trade_side, *path_far)
+    small_pass = remote(small.at[1], small.at[3], SIDE)
+    trade_pass = pieces(wall.at[1], wall.at[3], SIDE, trades)
+    path_pass = pieces(pall.at[2], pall.at[3], CORE, rows)
+    front = pl.ds(0, REGRESSORS)
+    design_core = remote(small.at[:, front], dall.at[0], CORE)
+    design_far = remote(small.at[:, front], dall.at[1], FAR)
+    design_pass = remote(dall.at[1], dall.at[2], CORE)
+
+    for load in loads[3:]:
+        load.wait()
+    labels = jnp.concatenate([set_ref[pl.ds(peers[s], 1), :] for s in trade_steps], axis=1)
+    table[...] = set_table(labels, set_total)
+
+    def value(first, last, left, right):
+        paths = pall[first:last].reshape((last - first) * rows, feats)
+        weights = wall[left:right].reshape((right - left) * trades, feats)
+        notional = jnp.concatenate(
+            [small[s, REGRESSORS:, :].astype(F32)[:1, :] for s in range(left, right)], axis=1
+        )
+        pre_act = mm(paths, weights, NT)
+        fade = jnp.exp(-jnp.abs(pre_act))
+        at = (slice(first * rows, last * rows), slice(left * trades, right * trades))
+        tval[at] = (notional * (jnp.maximum(pre_act, 0.0) + jnp.log1p(fade))).astype(BF16)
+        nsig[at] = notional * (jnp.where(pre_act >= 0.0, 1.0, fade) / (1.0 + fade))
+
+    arrive(small_near)
+    start(small_pass)
+    arrive(path_core)
+    place(1)
+    value(0, 2, 0, 1)
+    for copy, onward in zip(trade_near, trade_pass):
+        arrive(copy)
+        start(onward)
+    value(0, 2, 1, 2)
+    arrive(small_side, small_pass)
+    start(design_core, design_far)
+    arrive(trade_side)
+    value(0, 2, 2, 3)
+    for copy, onward in zip(path_far, path_pass):
+        arrive(copy)
+        start(onward)
+    place(2)
+    value(2, 3, 0, 3)
+    arrive(*trade_pass)
+    value(0, 3, 3, 4)
+    head = 3 * rows
+    by_trade = mm(dturn[:, :head], tval[:head, :])
+    arrive(design_far)
+    start(design_pass)
+    arrive(*path_pass)
+    place(3)
+    value(3, 4, 0, 4)
+    by_trade = by_trade + mm(dturn[:, head:], tval[head:, :])
+    by_set = mm(jnp.concatenate(split3(by_trade), axis=0), table[...], NT)
+    moments = (
+        by_set[:REGRESSORS] + by_set[REGRESSORS : 2 * REGRESSORS] + by_set[2 * REGRESSORS :]
+    )
+    for i in range(4):
+        bown[i] = moments[:, i * quarter : (i + 1) * quarter]
+    quads = (CORE + SIDE, SIDE, CORE)
+    lines = (NEAR + FAR, FAR, NEAR)
+
+    def total(ref, count):
+        result = ref[0].astype(F32)
+        for i in range(1, count):
+            result = result + ref[i].astype(F32)
+        return result
+
+    moment_q = grouped(lambda peer: bown.at[lax.rem(peer, 4)], bq.at[q], quads)
+    start(*moment_q)
+    bq[q] = bown[q]
+
+    arrive(design_core, design_pass)
+    for s in range(4):
+        dgrid[peers[trade_steps[s]]] = small[s, :REGRESSORS, :]
+    for k in range(1, 4):
+        for s in range(4):
+            dgrid[peers[trade_steps[s] + path_steps[k]]] = dall[k - 1, s]
+    turned_all = jnp.concatenate([dgrid[i] for i in range(16)], axis=1)
+    dstack[...] = jnp.concatenate(
+        [turned_all, turned_all, turned_all, jnp.zeros_like(turned_all)], axis=0
+    )
+    gram = mm(turned_all, turned_all, NT)
+    gram = jnp.concatenate([gram, jnp.zeros((REGRESSORS, LANES - REGRESSORS), F32)], axis=1)
+    gram_row = lax.broadcasted_iota(jnp.int32, (REGRESSORS, LANES), 0)
+    gram_lane = lax.broadcasted_iota(jnp.int32, (REGRESSORS, LANES), 1)
+    ridge = jnp.where(gram_row == gram_lane, RIDGE_SCALE * paths_all, 0.0)
+    work = eliminate(augmented(gram + ridge), 0, FIRST_STEPS)
+
+    arrive(*moment_q)
+    bzsend[...] = total(bq, 4)
+    moment_z = grouped(lambda peer: bzsend, bz.at[z], lines)
+    start(*moment_z)
+    bz[z] = bzsend[...]
+    work = eliminate(work, FIRST_STEPS, REGRESSORS)
+    invert[...] = pltpu.roll(work, LANES - REGRESSORS, 1)
+    all_levels = tidx_ref[...]
+    all_thresholds = jnp.zeros((4, quarter), F32)
+    levels = tidx_ref[pl.ds(q, 1), :]
+    thresholds = jnp.zeros((1, quarter), F32)
+    for i in range(level_ref.shape[0]):
+        thresholds = jnp.where(levels == i, level_ref[i], thresholds)
+        all_thresholds = jnp.where(all_levels == i, level_ref[i], all_thresholds)
+    thresholds = jnp.transpose(jnp.broadcast_to(thresholds, (quarter, quarter)))[:, :1]
+    rate = jnp.transpose(
+        jnp.broadcast_to(rate_ref[pl.ds(q, 1), :], (quarter, quarter))
+    )[:, :1]
+    all_rates = rate_ref[...]
+    full_thresholds = jnp.concatenate([all_thresholds[i : i + 1] for i in range(4)], axis=1)
+    full_rates = jnp.concatenate([all_rates[i : i + 1] for i in range(4)], axis=1)
+
+    arrive(*moment_z)
+    inverse = invert[:, :REGRESSORS]
+    coeffs = precise(inverse, total(bz, 4))
+    csend[...] = coeffs
+    coeffs_q = grouped(lambda peer: csend, cq.at[q], quads)
+    start(*coeffs_q)
+    cq[q] = coeffs
+    excess = mm(stack3(coeffs), dstack[...], TN) - thresholds
+    over_ref[...] = excess
+    fade = jnp.exp(-jnp.abs(excess))
+    seed = rate * (jnp.where(excess >= 0.0, 1.0, fade) / (1.0 + fade))
+    seed_cut = mm(dstack[:REGRESSORS, :], jnp.concatenate(split3(seed), axis=0), NT)
+    seed_sum = (
+        seed_cut[:, :quarter] + seed_cut[:, quarter : 2 * quarter] + seed_cut[:, 2 * quarter :]
+    )
+    solved = precise(inverse, seed_sum)
+    ssend[...] = solved
+    answer_q = grouped(lambda peer: ssend, sq.at[q], quads)
+    start(*answer_q)
+    sq[q] = solved
+
+    excess = over_ref[...]
+    loss = jnp.maximum(excess, 0.0) + jnp.log1p(jnp.exp(-jnp.abs(excess)))
+    loss_part = jnp.sum(rate * jnp.sum(loss, axis=1, keepdims=True), axis=0, keepdims=True)
+    lsend[...] = jnp.broadcast_to(loss_part, lsend.shape)
+    lq[q] = lsend[...]
+    loss_q = grouped(lambda peer: lsend, lq.at[q], quads)
+
+    arrive(*coeffs_q)
+    own_triple = dtri[:rows, :]
+    coeffs_all = jnp.concatenate([cq[i] for i in range(4)], axis=1)
+    fitted = mm(own_triple, stack3(coeffs_all))
+    over = fitted - full_thresholds
+    fall = jnp.exp(-jnp.abs(over))
+    own_seed = full_rates * (jnp.where(over >= 0.0, 1.0, fall) / (1.0 + fall))
+
+    arrive(*answer_q)
+    solved_all = jnp.concatenate([sq[i] for i in range(4)], axis=1)
+    picked = mm(jnp.concatenate(split3(solved_all), axis=0), table[...])
+    solved3 = jnp.concatenate(
+        [picked.astype(BF16), jnp.zeros((LANES - 3 * REGRESSORS, picked.shape[1]), BF16)], axis=0
+    )
+    spread = mm(dtri[...], solved3).astype(BF16).astype(F32)
+    slopes[...] = (nsig[...] * spread).astype(BF16)
+
+    scale = 1.0 / math.sqrt(paths_all)
+
+    def basis_part(first, last):
+        return mm(slopes[first * rows : last * rows, :], wall[...].reshape(4 * trades, feats))
+
+    def weight_part(left, right):
+        cut = slopes[:, left * trades : right * trades]
+        return mm(cut, pall[...].reshape(4 * rows, feats), TN) * scale
+
+    psend[0] = basis_part(3, 4).astype(BF16)
+    basis_via = pieces(psend.at[0], pvia, CORE, rows)
+    start(*basis_via)
+    part = weight_part(2, 4)
+    wsend[0] = part[trades:].astype(BF16)
+    weight_via = pieces(wsend.at[0], wvia, SIDE, trades)
+    start(*weight_via)
+    wsend[1] = part[:trades].astype(BF16)
+    weight_side = remote(wsend.at[1], wz.at[0], SIDE)
+    start(weight_side)
+    part = basis_part(1, 3)
+    psend[1] = part[:rows].astype(BF16)
+    basis_core = remote(psend.at[1], pq.at[0], CORE)
+    start(basis_core)
+    pfar[...] = part[rows:]
+    basis_far = pieces(pjoin, pq.at[1], FAR, rows)
+    for p, (copy, onward) in enumerate(zip(basis_via, basis_far)):
+        cut = slice(p * rows // PIECES, (p + 1) * rows // PIECES)
+        arrive(copy)
+        pjoin[cut, :] = (pfar[cut, :] + pvia[cut, :].astype(F32)).astype(BF16)
+        start(onward)
+    wnear[...] = weight_part(1, 2)
+    pulled = mm(solved3, tval[...], NT)
+    pulled = (
+        pulled[:REGRESSORS]
+        + pulled[REGRESSORS : 2 * REGRESSORS]
+        + pulled[2 * REGRESSORS : 3 * REGRESSORS]
+    )
+    esend[0] = pulled[:, 3 * rows :]
+    esend[1] = pulled[:, rows : 2 * rows]
+    pull_via = remote(esend.at[0], evia, CORE)
+    pull_core = remote(esend.at[1], eq.at[0], CORE)
+    pull_far = remote(ejoin, eq.at[1], FAR)
+    start(pull_via, pull_core, *loss_q)
+    weight_near = pieces(wjoin, wz.at[1], NEAR, trades)
+    for p, (copy, onward) in enumerate(zip(weight_via, weight_near)):
+        cut = slice(p * trades // PIECES, (p + 1) * trades // PIECES)
+        arrive(copy)
+        wjoin[cut, :] = (wnear[cut, :] + wvia[cut, :].astype(F32)).astype(BF16)
+        start(onward)
+        if p == 0:
+            arrive(pull_via)
+            ejoin[...] = pulled[:, 2 * rows : 3 * rows] + evia[...]
+            start(pull_far)
+    wadj_ref[...] = weight_part(0, 1)
+    basis_ref[...] = basis_part(0, 1)
+
+    residual = own_seed - mm(own_triple, stack3(solved_all))
+    term = precise(coeffs_all, residual, NT) - precise(solved_all, fitted, NT)
+    arrive(*loss_q)
+    answers = jnp.concatenate([lq[i] for i in range(4)], axis=1)
+    loss_sum = jnp.sum(answers[:1], axis=1, keepdims=True) / quarter
+    loss_ref[...] = jnp.broadcast_to(loss_sum / (paths_all * set_total), loss_ref.shape)
+    arrive(pull_core, pull_far)
+    term = term + pulled[:, :rows] + eq[0] + eq[1]
+    padded = jnp.concatenate([term, jnp.zeros((LANES - REGRESSORS, rows), F32)], axis=0)
+    turned = pltpu.roll(jnp.transpose(padded), LANES - 1, 1)
+    lane = lax.broadcasted_iota(jnp.int32, turned.shape, 1)
+    turned = jnp.where(lane < REGRESSORS - 1, turned, 0.0)
+    basis_ref[:, :LANES] = basis_ref[:, :LANES] + turned
+    arrive(basis_core, *basis_far)
+    basis_ref[...] = basis_ref[...] + (pq[0].astype(F32) + pq[1].astype(F32))
+    arrive(weight_side, *weight_near)
+    wadj_ref[...] = wadj_ref[...] + (wz[0].astype(F32) + wz[1].astype(F32))
+    for copy in copies:
+        copy.wait_send()
+
+
+def square_scratch(rows, trades, feats, set_total):
+    size, quarter = REGRESSORS, set_total // 4
+    return [
+        pltpu.VMEM((4, rows, feats), BF16),
+        pltpu.VMEM((4, trades, feats), BF16),
+        pltpu.VMEM((4, size + 16, trades), BF16),
+        pltpu.VMEM((3, 4, size, rows), BF16),
+        pltpu.VMEM((16, size, rows), BF16),
+        pltpu.VMEM((LANES, 16 * rows), BF16),
+        pltpu.VMEM((4 * rows, LANES), BF16),
+        pltpu.VMEM((size, 4 * rows), BF16),
+        pltpu.VMEM((set_total, 4 * trades), BF16),
+        pltpu.VMEM((size, LANES), F32),
+        pltpu.VMEM((4, size, quarter), F32),
+        pltpu.VMEM((4, size, quarter), F32),
+        pltpu.VMEM((size, quarter), F32),
+        pltpu.VMEM((4, size, quarter), F32),
+        pltpu.VMEM((size, quarter), F32),
+        pltpu.VMEM((4, size, quarter), F32),
+        pltpu.VMEM((size, quarter), F32),
+        pltpu.VMEM((4, size, quarter), F32),
+        pltpu.VMEM((8, quarter), F32),
+        pltpu.VMEM((4, 8, quarter), F32),
+        pltpu.VMEM((quarter, 16 * rows), F32),
+        pltpu.VMEM((4 * rows, 4 * trades), BF16),
+        pltpu.VMEM((4 * rows, 4 * trades), F32),
+        pltpu.VMEM((4 * rows, 4 * trades), BF16),
+        pltpu.VMEM((2, trades, feats), BF16),
+        pltpu.VMEM((trades, feats), BF16),
+        pltpu.VMEM((trades, feats), F32),
+        pltpu.VMEM((trades, feats), BF16),
+        pltpu.VMEM((2, trades, feats), BF16),
+        pltpu.VMEM((2, rows, feats), BF16),
+        pltpu.VMEM((rows, feats), BF16),
+        pltpu.VMEM((rows, feats), F32),
+        pltpu.VMEM((rows, feats), BF16),
+        pltpu.VMEM((2, rows, feats), BF16),
+        pltpu.VMEM((2, size, rows), F32),
+        pltpu.VMEM((size, rows), F32),
+        pltpu.VMEM((size, rows), F32),
+        pltpu.VMEM((2, size, rows), F32),
+        pltpu.SemaphoreType.DMA((7,)),
+        pltpu.SemaphoreType.DMA((COPIES,)),
+        pltpu.SemaphoreType.DMA((COPIES,)),
+    ]
+
+
+def chain_scratch(inner, outer, rows, trades, feats, set_total):
+    size, quarter, count = REGRESSORS, set_total // inner, inner * outer
+    z_pairs, q_pairs = max(outer - 1, 1), max(inner - 1, 1)
+    return [
+        pltpu.VMEM((inner, rows, feats), BF16),
+        pltpu.VMEM((outer, trades, feats), BF16),
+        pltpu.VMEM((outer, 8, trades), F32),
+        pltpu.VMEM((8, trades), F32),
+        pltpu.VMEM((size, rows), BF16),
+        pltpu.VMEM((outer, size, rows), BF16),
+        pltpu.VMEM((inner, outer, size, rows), BF16),
+        pltpu.VMEM((LANES, count * rows), BF16),
+        pltpu.VMEM((set_total, outer * trades), BF16),
+        pltpu.VMEM((size, LANES), F32),
+        pltpu.VMEM((inner, size, quarter), F32),
+        pltpu.VMEM((inner, size, quarter), F32),
+        pltpu.VMEM((size, quarter), F32),
+        pltpu.VMEM((outer, size, quarter), F32),
+        pltpu.VMEM((size, quarter), F32),
+        pltpu.VMEM((inner, size, quarter), F32),
+        pltpu.VMEM((size + 8, quarter), F32),
+        pltpu.VMEM((inner, size + 8, quarter), F32),
+        pltpu.VMEM((inner, size, rows), F32),
+        pltpu.VMEM((inner, size, rows), F32),
+        pltpu.VMEM((outer, trades, feats), BF16),
+        pltpu.VMEM((outer, trades, feats), BF16),
+        pltpu.VMEM((inner, rows, feats), BF16),
+        pltpu.VMEM((inner, rows, feats), BF16),
+        pltpu.VMEM((inner * rows, outer * trades), F32),
+        pltpu.VMEM((inner * rows, outer * trades), BF16),
+        pltpu.SemaphoreType.DMA((7,)),
+        pltpu.SemaphoreType.DMA((5, z_pairs)),
+        pltpu.SemaphoreType.DMA((5, z_pairs)),
+        pltpu.SemaphoreType.DMA((7, q_pairs)),
+        pltpu.SemaphoreType.DMA((7, q_pairs)),
+    ]
 
 
 def shards(
@@ -450,11 +763,15 @@
     trades = proxy_weight.shape[0]
     set_total = loss_rate.shape[0]
     quarter = set_total // inner
-    size = REGRESSORS
     vmem = pl.BlockSpec(memory_space=pltpu.VMEM)
-    z_pairs, q_pairs = max(outer - 1, 1), max(inner - 1, 1)
+    if count == 16 and rows == trades and rows % (16 * PIECES) == 0:
+        body = functools.partial(square, rows * count, set_total)
+        scratch = square_scratch(rows, trades, feats, set_total)
+    else:
+        body = functools.partial(kernel, inner, outer, rows * count, set_total)
+        scratch = chain_scratch(inner, outer, rows, trades, feats, set_total)
     loss, basis_adjoint, weight_adjoint = pl.pallas_call(
-        functools.partial(kernel, inner, outer, rows * count, set_total),
+        body,
         out_shape=(
             jax.ShapeDtypeStruct((1, LANES), F32),
             jax.ShapeDtypeStruct((rows, feats), F32),
@@ -468,39 +785,7 @@
             pltpu.VMEM((inner, quarter), jnp.int32),
             pltpu.SMEM(threshold_levels.shape, F32),
             pltpu.VMEM((inner, quarter), F32),
-            pltpu.VMEM((inner, rows, feats), BF16),
-            pltpu.VMEM((outer, trades, feats), BF16),
-            pltpu.VMEM((outer, 8, trades), F32),
-            pltpu.VMEM((8, trades), F32),
-            pltpu.VMEM((size, rows), BF16),
-            pltpu.VMEM((outer, size, rows), BF16),
-            pltpu.VMEM((inner, outer, size, rows), BF16),
-            pltpu.VMEM((LANES, count * rows), BF16),
-            pltpu.VMEM((set_total, outer * trades), BF16),
-            pltpu.VMEM((size, LANES), F32),
-            pltpu.VMEM((inner, size, quarter), F32),
-            pltpu.VMEM((inner, size, quarter), F32),
-            pltpu.VMEM((size, quarter), F32),
-            pltpu.VMEM((outer, size, quarter), F32),
-            pltpu.VMEM((size, quarter), F32),
-            pltpu.VMEM((inner, size, quarter), F32),
-            pltpu.VMEM((size + 8, quarter), F32),
-            pltpu.VMEM((inner, size + 8, quarter), F32),
-            pltpu.VMEM((inner, size, rows), F32),
-            pltpu.VMEM((inner, size, rows), F32),
-            pltpu.VMEM((outer, trades, feats), BF16),
-            pltpu.VMEM((outer, trades, feats), BF16),
-            pltpu.VMEM((inner, rows, feats), BF16),
-            pltpu.VMEM((inner, rows, feats), BF16),
-            pltpu.VMEM((inner * rows, outer * trades), F32),
-            pltpu.VMEM((inner * rows, outer * trades), BF16),
-            pltpu.VMEM((trades, feats), BF16),
-            pltpu.SemaphoreType.DMA((7,)),
-            pltpu.SemaphoreType.DMA((5, z_pairs)),
-            pltpu.SemaphoreType.DMA((5, z_pairs)),
-            pltpu.SemaphoreType.DMA((7, q_pairs)),
-            pltpu.SemaphoreType.DMA((7, q_pairs)),
-            pltpu.SemaphoreType.DMA((8, PIECES)),
+            *scratch,
         ],
         compiler_params=pltpu.CompilerParams(
             collective_id=0, has_side_effects=True, vmem_limit_bytes=48 * 1024 * 1024

time: 45.9 us -> 45 us (0.980)
  Pallas kernels: 42.6 us -> 41.6 us
    pallas_call x1, Pallas kernels: 42.6 us -> 41.6 us  [shards(): pl.pallas_call(body, out_shape=(jax.ShapeDtypeStruct((1, LANES), F32), ja...]
where the time goes in v1:
time: 45 us; the launch traced here: 44.8 us
  Pallas kernels  41.6 us (92%)
  between operations  1.8 us (4%)
  local copies, waits for them, and re-layouts  1.41 us (3%)
    pallas_call x1, Pallas kernels, shards(): pl.pallas_call(body, out_shape=(jax.ShapeDtypeStruct((1, LANES), F32), ja...  41.6 us
    unnamed x2, local copies, waits for them, and re-layouts  1.41 us

profile of v1, /device:TPU:0, one launch (start us, length us, event | category | flops | bytes accessed | tf_op | source)
XLA Modules:
  0.0 44.8 jit_solution(14898730412809557558)
XLA Ops:
  0.6 41.6 %shard_map.94 = (f32[1,128]{1,0:T(1,128)S(1)}, f32[128,512]{1,0:T(8,128)S(1)}, f32[128,512]{1,0:T(8,128)S(1)}) custom-call(bf16[128,512]{1,0:T(8,128)(2,1)} %pb_hbm.1, bf16[128,512]{1,0:T(8,128)(2,1)} %w_hbm.1, bf16[1,128]{1,0:T(2,128)(2,1)} %bitcast.10, s32[16,128]{1,0:T(8,128)} %bitcast.7, s32[4,128]{1,0:T(4,128)} %bitcast.8, f32[16]{0:T(128)} %level_hbm.1, ...), custom_call_target="tpu_custom_call" | custom-call | tf_op jit(solution)/shard_map/pallas_call | solution.py:773
  42.3 0.7 %copy.14 = f32[128,512]{1,0:T(8,128)} copy(f32[128,512]{1,0:T(8,128)S(1)} %get-tuple-element.13) | data formatting | bytes 524288
  43.0 0.7 %copy.15 = f32[128,512]{1,0:T(8,128)} copy(f32[128,512]{1,0:T(8,128)S(1)} %get-tuple-element.14) | data formatting | bytes 524288

commit v2 on v1

--- a/solution.py
+++ b/solution.py
@@ -13,7 +13,7 @@
 PRECISE = lax.Precision.HIGHEST
 LANES = 128
 PIECES = 4
-FIRST_STEPS = 12
+FIRST_STEPS = 10
 COPIES = 64
 F32 = jnp.float32
 BF16 = jnp.bfloat16
@@ -350,15 +350,16 @@
     bown, bq, bzsend, bz, csend, cq, ssend, sq, lsend, lq, over_ref,
     tval, nsig, slopes,
     wsend, wvia, wnear, wjoin, wz, psend, pvia, pfar, pjoin, pq, esend, evia, ejoin, eq,
-    local, send, recv,
+    local, send, recv, ready, order,
 ):
     rows, feats = basis_ref.shape
     trades = wadj_ref.shape[0]
     quarter = set_total // 4
     me = lax.axis_index("paths")
     q, z = lax.rem(me, 4), lax.div(me, 4)
+    bits = [lax.rem(lax.div(me, weight), 2) for weight in (1, 2, 4, 8)]
     peers = [me] + [partner(me, step, 16) for step in range(1, 16)]
-    CORE, SIDE, NEAR, FAR = 1, 2, 4, 8
+    CORE, SIDE, NEAR, FAR = around = 1, 2, 4, 8
     trade_steps = (0, NEAR, SIDE, NEAR + SIDE)
     path_steps = (0, CORE, FAR, CORE + FAR)
 
@@ -366,7 +367,7 @@
         pltpu.make_async_copy(source, target, local.at[i])
         for i, (source, target) in enumerate(
             [
-                (pb_hbm, pall.at[0]),
+                (pb_hbm, pall.at[pl.ds(0 * rows, rows)]),
                 (not_hbm, not_ref),
                 (w_hbm, wall.at[0]),
                 (set_hbm, set_ref),
@@ -377,11 +378,19 @@
         )
     ]
     barrier = pltpu.get_barrier_semaphore()
-    for step in (CORE, SIDE, NEAR, FAR):
+
+    def greet(semaphore, step):
         pl.semaphore_signal(
-            barrier, inc=1, device_id={"paths": peers[step]},
+            semaphore, inc=1, device_id={"paths": peers[step]},
             device_id_type=pl.DeviceIdType.MESH,
         )
+
+    for i, step in enumerate(around):
+
+        @pl.when(bits[i] == 0)
+        def _():
+            greet(barrier, step)
+
     for load in loads:
         load.start()
 
@@ -400,6 +409,10 @@
         for copy in group:
             copy.start()
 
+    def fence():
+        pl.semaphore_signal(order, inc=1)
+        pl.semaphore_wait(order, 1)
+
     def arrive(*group):
         for copy in group:
             copy.wait_recv()
@@ -413,31 +426,61 @@
         return [remote(source(peers[s]), target, s) for s in bits]
 
     def place(i):
-        design = design_of(pall[i])
+        design = design_of(pall[i * rows : (i + 1) * rows, :])
         at = slice(i * rows, (i + 1) * rows)
         dtri[at, :] = triple(design)
         turned = jnp.transpose(design)[:REGRESSORS, :].astype(BF16)
         dturn[:, at] = turned
         return turned
 
+    path_core = remote(pb_hbm, pall.at[pl.ds(1 * rows, rows)], CORE)
+    trade_side = remote(w_hbm, wall.at[2], SIDE)
+    trade_near = pieces(w_hbm, wall.at[1], NEAR, trades)
+    path_far = pieces(pb_hbm, pall.at[pl.ds(2 * rows, rows)], FAR, rows)
+    small_side = remote(small.at[0], small.at[2], SIDE)
+    small_near = remote(small.at[0], small.at[1], NEAR)
+
+    lower = bits[0] + bits[1] + bits[2] + bits[3]
+
+    @pl.when(lower > 0)
+    def _():
+        pl.semaphore_wait(barrier, lower)
+
+    for i, step in enumerate(around):
+
+        @pl.when(bits[i] == 1)
+        def _():
+            greet(ready.at[i], step)
+
+    def down(i, *group):
+        @pl.when(bits[i] == 1)
+        def _():
+            start(*group)
+
+    def up(i, *group):
+        @pl.when(bits[i] == 0)
+        def _():
+            pl.semaphore_wait(ready.at[i], 1)
+            start(*group)
+
+    down(2, *trade_near)
+    down(1, trade_side)
+    down(0, path_core)
     loads[0].wait()
     own_turned = place(0)
     loads[1].wait()
     note = jnp.broadcast_to(not_ref[...].astype(F32), (16, trades)).astype(BF16)
     small[0] = jnp.concatenate([own_turned, note], axis=0)
+    up(0, path_core)
+    up(1, trade_side)
+    start(small_side)
+    up(2, *trade_near)
+    start(small_near)
+    up(3)
     loads[2].wait()
-    pl.semaphore_wait(barrier, 4)
-
-    small_near = remote(small.at[0], small.at[1], NEAR)
-    small_side = remote(small.at[0], small.at[2], SIDE)
-    trade_near = pieces(wall.at[0], wall.at[1], NEAR, trades)
-    path_core = remote(pall.at[0], pall.at[1], CORE)
-    trade_side = remote(wall.at[0], wall.at[2], SIDE)
-    path_far = pieces(pall.at[0], pall.at[2], FAR, rows)
-    start(small_near, small_side, *trade_near, path_core, trade_side, *path_far)
     small_pass = remote(small.at[1], small.at[3], SIDE)
     trade_pass = pieces(wall.at[1], wall.at[3], SIDE, trades)
-    path_pass = pieces(pall.at[2], pall.at[3], CORE, rows)
+    path_pass = pieces(pall.at[pl.ds(2 * rows, rows)], pall.at[pl.ds(3 * rows, rows)], CORE, rows)
     front = pl.ds(0, REGRESSORS)
     design_core = remote(small.at[:, front], dall.at[0], CORE)
     design_far = remote(small.at[:, front], dall.at[1], FAR)
@@ -448,45 +491,46 @@
     labels = jnp.concatenate([set_ref[pl.ds(peers[s], 1), :] for s in trade_steps], axis=1)
     table[...] = set_table(labels, set_total)
 
-    def value(first, last, left, right):
-        paths = pall[first:last].reshape((last - first) * rows, feats)
+    def value(top, bottom, left, right):
+        paths = pall[top:bottom, :]
         weights = wall[left:right].reshape((right - left) * trades, feats)
         notional = jnp.concatenate(
             [small[s, REGRESSORS:, :].astype(F32)[:1, :] for s in range(left, right)], axis=1
         )
         pre_act = mm(paths, weights, NT)
         fade = jnp.exp(-jnp.abs(pre_act))
-        at = (slice(first * rows, last * rows), slice(left * trades, right * trades))
+        at = (slice(top, bottom), slice(left * trades, right * trades))
         tval[at] = (notional * (jnp.maximum(pre_act, 0.0) + jnp.log1p(fade))).astype(BF16)
         nsig[at] = notional * (jnp.where(pre_act >= 0.0, 1.0, fade) / (1.0 + fade))
 
+    pair, head = 2 * rows, 3 * rows
+    arrive(path_core)
+    place(1)
+    for p, (copy, onward) in enumerate(zip(trade_near, trade_pass)):
+        arrive(copy)
+        start(onward)
+        if p == 0:
+            start(*path_far)
     arrive(small_near)
     start(small_pass)
-    arrive(path_core)
-    place(1)
-    value(0, 2, 0, 1)
-    for copy, onward in zip(trade_near, trade_pass):
-        arrive(copy)
-        start(onward)
-    value(0, 2, 1, 2)
-    arrive(small_side, small_pass)
-    start(design_core, design_far)
-    arrive(trade_side)
-    value(0, 2, 2, 3)
+    greet(ready.at[4], FAR)
+    arrive(trade_side, small_side)
+    value(0, pair, 0, 3)
     for copy, onward in zip(path_far, path_pass):
         arrive(copy)
         start(onward)
+    fence()
     place(2)
-    value(2, 3, 0, 3)
+    value(pair, head, 0, 3)
+    arrive(small_pass)
+    start(design_core, design_far)
+    fence()
     arrive(*trade_pass)
-    value(0, 3, 3, 4)
-    head = 3 * rows
+    value(0, head, 3, 4)
     by_trade = mm(dturn[:, :head], tval[:head, :])
-    arrive(design_far)
-    start(design_pass)
     arrive(*path_pass)
     place(3)
-    value(3, 4, 0, 4)
+    value(head, 4 * rows, 0, 4)
     by_trade = by_trade + mm(dturn[:, head:], tval[head:, :])
     by_set = mm(jnp.concatenate(split3(by_trade), axis=0), table[...], NT)
     moments = (
@@ -505,8 +549,12 @@
 
     moment_q = grouped(lambda peer: bown.at[lax.rem(peer, 4)], bq.at[q], quads)
     start(*moment_q)
+    fence()
     bq[q] = bown[q]
 
+    arrive(design_far)
+    start(design_pass)
+    fence()
     arrive(design_core, design_pass)
     for s in range(4):
         dgrid[peers[trade_steps[s]]] = small[s, :REGRESSORS, :]
@@ -526,8 +574,10 @@
 
     arrive(*moment_q)
     bzsend[...] = total(bq, 4)
+    pl.semaphore_wait(ready.at[4], 1)
     moment_z = grouped(lambda peer: bzsend, bz.at[z], lines)
     start(*moment_z)
+    fence()
     bz[z] = bzsend[...]
     work = eliminate(work, FIRST_STEPS, REGRESSORS)
     invert[...] = pltpu.roll(work, LANES - REGRESSORS, 1)
@@ -551,7 +601,6 @@
     coeffs = precise(inverse, total(bz, 4))
     csend[...] = coeffs
     coeffs_q = grouped(lambda peer: csend, cq.at[q], quads)
-    start(*coeffs_q)
     cq[q] = coeffs
     excess = mm(stack3(coeffs), dstack[...], TN) - thresholds
     over_ref[...] = excess
@@ -565,6 +614,8 @@
     ssend[...] = solved
     answer_q = grouped(lambda peer: ssend, sq.at[q], quads)
     start(*answer_q)
+    start(*coeffs_q)
+    fence()
     sq[q] = solved
 
     excess = over_ref[...]
@@ -573,14 +624,8 @@
     lsend[...] = jnp.broadcast_to(loss_part, lsend.shape)
     lq[q] = lsend[...]
     loss_q = grouped(lambda peer: lsend, lq.at[q], quads)
-
-    arrive(*coeffs_q)
-    own_triple = dtri[:rows, :]
-    coeffs_all = jnp.concatenate([cq[i] for i in range(4)], axis=1)
-    fitted = mm(own_triple, stack3(coeffs_all))
-    over = fitted - full_thresholds
-    fall = jnp.exp(-jnp.abs(over))
-    own_seed = full_rates * (jnp.where(over >= 0.0, 1.0, fall) / (1.0 + fall))
+    start(*loss_q)
+    fence()
 
     arrive(*answer_q)
     solved_all = jnp.concatenate([sq[i] for i in range(4)], axis=1)
@@ -588,8 +633,10 @@
     solved3 = jnp.concatenate(
         [picked.astype(BF16), jnp.zeros((LANES - 3 * REGRESSORS, picked.shape[1]), BF16)], axis=0
     )
-    spread = mm(dtri[...], solved3).astype(BF16).astype(F32)
-    slopes[...] = (nsig[...] * spread).astype(BF16)
+
+    def slope(top, bottom):
+        spread = mm(dtri[top:bottom, :], solved3).astype(BF16).astype(F32)
+        slopes[top:bottom, :] = (nsig[top:bottom, :] * spread).astype(BF16)
 
     scale = 1.0 / math.sqrt(paths_all)
 
@@ -598,11 +645,14 @@
 
     def weight_part(left, right):
         cut = slopes[:, left * trades : right * trades]
-        return mm(cut, pall[...].reshape(4 * rows, feats), TN) * scale
-
+        return mm(cut, pall[...], TN) * scale
+
+    slope(head, 4 * rows)
     psend[0] = basis_part(3, 4).astype(BF16)
     basis_via = pieces(psend.at[0], pvia, CORE, rows)
     start(*basis_via)
+    fence()
+    slope(0, head)
     part = weight_part(2, 4)
     wsend[0] = part[trades:].astype(BF16)
     weight_via = pieces(wsend.at[0], wvia, SIDE, trades)
@@ -610,10 +660,8 @@
     wsend[1] = part[:trades].astype(BF16)
     weight_side = remote(wsend.at[1], wz.at[0], SIDE)
     start(weight_side)
+    fence()
     part = basis_part(1, 3)
-    psend[1] = part[:rows].astype(BF16)
-    basis_core = remote(psend.at[1], pq.at[0], CORE)
-    start(basis_core)
     pfar[...] = part[rows:]
     basis_far = pieces(pjoin, pq.at[1], FAR, rows)
     for p, (copy, onward) in enumerate(zip(basis_via, basis_far)):
@@ -621,6 +669,11 @@
         arrive(copy)
         pjoin[cut, :] = (pfar[cut, :] + pvia[cut, :].astype(F32)).astype(BF16)
         start(onward)
+        fence()
+    psend[1] = part[:rows].astype(BF16)
+    basis_core = remote(psend.at[1], pq.at[0], CORE)
+    start(basis_core)
+    fence()
     wnear[...] = weight_part(1, 2)
     pulled = mm(solved3, tval[...], NT)
     pulled = (
@@ -633,7 +686,8 @@
     pull_via = remote(esend.at[0], evia, CORE)
     pull_core = remote(esend.at[1], eq.at[0], CORE)
     pull_far = remote(ejoin, eq.at[1], FAR)
-    start(pull_via, pull_core, *loss_q)
+    start(pull_via, pull_core)
+    fence()
     weight_near = pieces(wjoin, wz.at[1], NEAR, trades)
     for p, (copy, onward) in enumerate(zip(weight_via, weight_near)):
         cut = slice(p * trades // PIECES, (p + 1) * trades // PIECES)
@@ -644,26 +698,41 @@
             arrive(pull_via)
             ejoin[...] = pulled[:, 2 * rows : 3 * rows] + evia[...]
             start(pull_far)
+    fence()
     wadj_ref[...] = weight_part(0, 1)
     basis_ref[...] = basis_part(0, 1)
 
+    arrive(*coeffs_q)
+    own_triple = dtri[:rows, :]
+    coeffs_all = jnp.concatenate([cq[i] for i in range(4)], axis=1)
+    fitted = mm(own_triple, stack3(coeffs_all))
+    over = fitted - full_thresholds
+    fall = jnp.exp(-jnp.abs(over))
+    own_seed = full_rates * (jnp.where(over >= 0.0, 1.0, fall) / (1.0 + fall))
     residual = own_seed - mm(own_triple, stack3(solved_all))
     term = precise(coeffs_all, residual, NT) - precise(solved_all, fitted, NT)
+    term = term + pulled[:, :rows]
     arrive(*loss_q)
     answers = jnp.concatenate([lq[i] for i in range(4)], axis=1)
     loss_sum = jnp.sum(answers[:1], axis=1, keepdims=True) / quarter
     loss_ref[...] = jnp.broadcast_to(loss_sum / (paths_all * set_total), loss_ref.shape)
+    arrive(basis_core)
+    basis_ref[...] = basis_ref[...] + pq[0].astype(F32)
+    arrive(weight_side)
+    wadj_ref[...] = wadj_ref[...] + wz[0].astype(F32)
+    arrive(*basis_far)
+    basis_ref[...] = basis_ref[...] + pq[1].astype(F32)
     arrive(pull_core, pull_far)
-    term = term + pulled[:, :rows] + eq[0] + eq[1]
+    term = term + eq[0] + eq[1]
     padded = jnp.concatenate([term, jnp.zeros((LANES - REGRESSORS, rows), F32)], axis=0)
     turned = pltpu.roll(jnp.transpose(padded), LANES - 1, 1)
     lane = lax.broadcasted_iota(jnp.int32, turned.shape, 1)
     turned = jnp.where(lane < REGRESSORS - 1, turned, 0.0)
     basis_ref[:, :LANES] = basis_ref[:, :LANES] + turned
-    arrive(basis_core, *basis_far)
-    basis_ref[...] = basis_ref[...] + (pq[0].astype(F32) + pq[1].astype(F32))
-    arrive(weight_side, *weight_near)
-    wadj_ref[...] = wadj_ref[...] + (wz[0].astype(F32) + wz[1].astype(F32))
+    for p, copy in enumerate(weight_near):
+        cut = slice(p * trades // PIECES, (p + 1) * trades // PIECES)
+        arrive(copy)
+        wadj_ref[cut, :] = wadj_ref[cut, :] + wz[1, cut, :].astype(F32)
     for copy in copies:
         copy.wait_send()
 
@@ -671,7 +740,7 @@
 def square_scratch(rows, trades, feats, set_total):
     size, quarter = REGRESSORS, set_total // 4
     return [
-        pltpu.VMEM((4, rows, feats), BF16),
+        pltpu.VMEM((4 * rows, feats), BF16),
         pltpu.VMEM((4, trades, feats), BF16),
         pltpu.VMEM((4, size + 16, trades), BF16),
         pltpu.VMEM((3, 4, size, rows), BF16),
@@ -712,6 +781,8 @@
         pltpu.SemaphoreType.DMA((7,)),
         pltpu.SemaphoreType.DMA((COPIES,)),
         pltpu.SemaphoreType.DMA((COPIES,)),
+        pltpu.SemaphoreType.REGULAR((5,)),
+        pltpu.SemaphoreType.REGULAR,
     ]
 
 

time: 45 us -> 42.5 us (0.944)
  Pallas kernels: 41.6 us -> 39.2 us
    pallas_call x1, Pallas kernels: 41.6 us -> 39.2 us  [shards(): pl.pallas_call(body, out_shape=(jax.ShapeDtypeStruct((1, LANES), F32), ja...]
where the time goes in v2:
time: 42.5 us; the launch traced here: 42.4 us
  Pallas kernels  39.2 us (92%)
  between operations  1.8 us (4%)
  local copies, waits for them, and re-layouts  1.41 us (3%)
    pallas_call x1, Pallas kernels, shards(): pl.pallas_call(body, out_shape=(jax.ShapeDtypeStruct((1, LANES), F32), ja...  39.2 us
    unnamed x2, local copies, waits for them, and re-layouts  1.41 us

profile of v2, /device:TPU:0, one launch (start us, length us, event | category | flops | bytes accessed | tf_op | source)
XLA Modules:
  0.0 42.4 jit_solution(3627695340336853524)
XLA Ops:
  0.6 39.2 %shard_map.94 = (f32[1,128]{1,0:T(1,128)S(1)}, f32[128,512]{1,0:T(8,128)S(1)}, f32[128,512]{1,0:T(8,128)S(1)}) custom-call(bf16[128,512]{1,0:T(8,128)(2,1)} %pb_hbm.1, bf16[128,512]{1,0:T(8,128)(2,1)} %w_hbm.1, bf16[1,128]{1,0:T(2,128)(2,1)} %bitcast.10, s32[16,128]{1,0:T(8,128)} %bitcast.7, s32[4,128]{1,0:T(4,128)} %bitcast.8, f32[16]{0:T(128)} %level_hbm.1, ...), custom_call_target="tpu_custom_call" | custom-call | tf_op jit(solution)/shard_map/pallas_call | solution.py:844
  39.8 0.7 %copy.14 = f32[128,512]{1,0:T(8,128)} copy(f32[128,512]{1,0:T(8,128)S(1)} %get-tuple-element.13) | data formatting | bytes 524288
  40.5 0.7 %copy.15 = f32[128,512]{1,0:T(8,128)} copy(f32[128,512]{1,0:T(8,128)S(1)} %get-tuple-element.14) | data formatting | bytes 524288

commit v3 on v2

--- a/solution.py
+++ b/solution.py
@@ -14,7 +14,7 @@
 LANES = 128
 PIECES = 4
 FIRST_STEPS = 10
-COPIES = 64
+COPIES = 96
 F32 = jnp.float32
 BF16 = jnp.bfloat16
 
@@ -348,8 +348,8 @@
     not_ref, set_ref, tidx_ref, level_ref, rate_ref,
     pall, wall, small, dall, dgrid, dstack, dtri, dturn, table, invert,
     bown, bq, bzsend, bz, csend, cq, ssend, sq, lsend, lq, over_ref,
-    tval, nsig, slopes,
-    wsend, wvia, wnear, wjoin, wz, psend, pvia, pfar, pjoin, pq, esend, evia, ejoin, eq,
+    by_trades, tval, nsig, slopes, pulls,
+    wsend, wvia, wnear, wjoin, wz, psend, pvia, pown, pjoin, pq, esend, evia, ejoin, eq,
     local, send, recv, ready, order,
 ):
     rows, feats = basis_ref.shape
@@ -359,15 +359,18 @@
     q, z = lax.rem(me, 4), lax.div(me, 4)
     bits = [lax.rem(lax.div(me, weight), 2) for weight in (1, 2, 4, 8)]
     peers = [me] + [partner(me, step, 16) for step in range(1, 16)]
-    CORE, SIDE, NEAR, FAR = around = 1, 2, 4, 8
+    low, high = bits[2], bits[3]
+    inner = low + high - 2 * low * high
+    CORE, SIDE, NEAR, FAR = 1, 2, 4, 8
+    MID = NEAR + FAR
     trade_steps = (0, NEAR, SIDE, NEAR + SIDE)
-    path_steps = (0, CORE, FAR, CORE + FAR)
+    design_steps = (0, CORE, FAR, CORE + FAR)
 
     loads = [
         pltpu.make_async_copy(source, target, local.at[i])
         for i, (source, target) in enumerate(
             [
-                (pb_hbm, pall.at[pl.ds(0 * rows, rows)]),
+                (pb_hbm, pall.at[pl.ds(0, rows)]),
                 (not_hbm, not_ref),
                 (w_hbm, wall.at[0]),
                 (set_hbm, set_ref),
@@ -385,25 +388,33 @@
             device_id_type=pl.DeviceIdType.MESH,
         )
 
-    for i, step in enumerate(around):
+    for i, step in enumerate((CORE, SIDE, NEAR, FAR)):
 
         @pl.when(bits[i] == 0)
         def _():
             greet(barrier, step)
 
+    @pl.when(inner * (1 - high) == 1)
+    def _():
+        greet(barrier, MID)
+
     for load in loads:
         load.start()
 
-    copies = []
-
-    def remote(source, target, step):
-        k = len(copies)
+    made, copies, inner_copies, outer_copies = [], [], [], []
+
+    def remote(source, target, step, bag=copies):
+        k = len(made)
         copy = pltpu.make_async_remote_copy(
             src_ref=source, dst_ref=target, send_sem=send.at[k], recv_sem=recv.at[k],
             device_id={"paths": peers[step]}, device_id_type=pl.DeviceIdType.MESH,
         )
-        copies.append(copy)
+        made.append(copy)
+        bag.append(copy)
         return copy
+
+    def slot(i):
+        return pall.at[pl.ds(i * rows, rows)]
 
     def start(*group):
         for copy in group:
@@ -417,10 +428,10 @@
         for copy in group:
             copy.wait_recv()
 
-    def pieces(source, target, step, extent):
+    def pieces(source, target, step, extent, bag=copies):
         part = extent // PIECES
         cuts = [pl.ds(p * part, part) for p in range(PIECES)]
-        return [remote(source.at[cut], target.at[cut], step) for cut in cuts]
+        return [remote(source.at[cut], target.at[cut], step, bag) for cut in cuts]
 
     def grouped(source, target, bits):
         return [remote(source(peers[s]), target, s) for s in bits]
@@ -433,24 +444,30 @@
         dturn[:, at] = turned
         return turned
 
-    path_core = remote(pb_hbm, pall.at[pl.ds(1 * rows, rows)], CORE)
-    trade_side = remote(w_hbm, wall.at[2], SIDE)
+    path_core = remote(pb_hbm, slot(1), CORE)
+    trade_side = pieces(w_hbm, wall.at[2], SIDE, trades)
     trade_near = pieces(w_hbm, wall.at[1], NEAR, trades)
-    path_far = pieces(pb_hbm, pall.at[pl.ds(2 * rows, rows)], FAR, rows)
+    path_mid = pieces(pb_hbm, slot(2), MID, rows, inner_copies)
+    path_far = pieces(pb_hbm, slot(4), FAR, rows, outer_copies)
     small_side = remote(small.at[0], small.at[2], SIDE)
     small_near = remote(small.at[0], small.at[1], NEAR)
 
-    lower = bits[0] + bits[1] + bits[2] + bits[3]
+    lower = bits[0] + bits[1] + bits[2] + bits[3] + inner * high
 
     @pl.when(lower > 0)
     def _():
         pl.semaphore_wait(barrier, lower)
 
-    for i, step in enumerate(around):
+    for i, step in enumerate((CORE, SIDE, NEAR)):
 
         @pl.when(bits[i] == 1)
         def _():
             greet(ready.at[i], step)
+
+    @pl.when(inner * high == 1)
+    def _():
+        greet(ready.at[3], FAR)
+        greet(ready.at[5], MID)
 
     def down(i, *group):
         @pl.when(bits[i] == 1)
@@ -463,24 +480,45 @@
             pl.semaphore_wait(ready.at[i], 1)
             start(*group)
 
-    down(2, *trade_near)
-    down(1, trade_side)
+    split = PIECES // 2
+    down(2, *trade_near[:split])
+
+    @pl.when(inner * high == 1)
+    def _():
+        start(*path_mid)
+
+    down(1, *trade_side[:split])
     down(0, path_core)
     loads[0].wait()
     own_turned = place(0)
     loads[1].wait()
     note = jnp.broadcast_to(not_ref[...].astype(F32), (16, trades)).astype(BF16)
     small[0] = jnp.concatenate([own_turned, note], axis=0)
+    down(2, small_near, *trade_near[split:])
+    down(1, small_side, *trade_side[split:])
     up(0, path_core)
-    up(1, trade_side)
-    start(small_side)
-    up(2, *trade_near)
-    start(small_near)
-    up(3)
+    up(1, small_side, *trade_side)
+    up(2, small_near, *trade_near)
+
+    @pl.when((1 - inner) * high == 1)
+    def _():
+        start(*path_far)
+
+    @pl.when(inner * (1 - high) == 1)
+    def _():
+        pl.semaphore_wait(ready.at[5], 1)
+        start(*path_mid)
+
+    @pl.when((1 - inner) * (1 - high) == 1)
+    def _():
+        pl.semaphore_wait(ready.at[3], 1)
+        start(*path_far)
+
     loads[2].wait()
     small_pass = remote(small.at[1], small.at[3], SIDE)
     trade_pass = pieces(wall.at[1], wall.at[3], SIDE, trades)
-    path_pass = pieces(pall.at[pl.ds(2 * rows, rows)], pall.at[pl.ds(3 * rows, rows)], CORE, rows)
+    mid_pass = pieces(slot(2), slot(3), CORE, rows, inner_copies)
+    far_pass = pieces(slot(4), slot(5), CORE, rows, inner_copies)
     front = pl.ds(0, REGRESSORS)
     design_core = remote(small.at[:, front], dall.at[0], CORE)
     design_far = remote(small.at[:, front], dall.at[1], FAR)
@@ -501,37 +539,69 @@
         fade = jnp.exp(-jnp.abs(pre_act))
         at = (slice(top, bottom), slice(left * trades, right * trades))
         tval[at] = (notional * (jnp.maximum(pre_act, 0.0) + jnp.log1p(fade))).astype(BF16)
-        nsig[at] = notional * (jnp.where(pre_act >= 0.0, 1.0, fade) / (1.0 + fade))
-
-    pair, head = 2 * rows, 3 * rows
+        nsig[at] = pre_act
+
+    def sigmoid(top, bottom):
+        notional = jnp.concatenate(
+            [small[s, REGRESSORS:, :].astype(F32)[:1, :] for s in range(4)], axis=1
+        )
+        pre_act = nsig[top:bottom, :]
+        fade = jnp.exp(-jnp.abs(pre_act))
+        nsig[top:bottom, :] = notional * (jnp.where(pre_act >= 0.0, 1.0, fade) / (1.0 + fade))
+
+    pair, head, tail, last = 2 * rows, 4 * rows, 5 * rows, 6 * rows
     arrive(path_core)
     place(1)
+
+    @pl.when(inner == 1)
+    def _():
+        for copy, onward in zip(path_mid, mid_pass):
+            arrive(copy)
+            start(onward)
+
     for p, (copy, onward) in enumerate(zip(trade_near, trade_pass)):
+        if p == split:
+            arrive(small_near)
+            start(small_pass)
         arrive(copy)
         start(onward)
-        if p == 0:
-            start(*path_far)
-    arrive(small_near)
-    start(small_pass)
-    greet(ready.at[4], FAR)
-    arrive(trade_side, small_side)
+    arrive(*trade_side, small_side)
     value(0, pair, 0, 3)
-    for copy, onward in zip(path_far, path_pass):
-        arrive(copy)
-        start(onward)
-    fence()
-    place(2)
-    value(pair, head, 0, 3)
+
+    @pl.when(inner == 1)
+    def _():
+        place(2)
+        arrive(*mid_pass)
+        place(3)
+        value(pair, head, 0, 3)
+        for copy, onward in zip(path_far, far_pass):
+            arrive(copy)
+            start(onward)
+        greet(ready.at[4], FAR)
+        fence()
+        place(4)
+        value(head, tail, 0, 3)
+
     arrive(small_pass)
     start(design_core, design_far)
     fence()
     arrive(*trade_pass)
-    value(0, head, 3, 4)
-    by_trade = mm(dturn[:, :head], tval[:head, :])
-    arrive(*path_pass)
-    place(3)
-    value(head, 4 * rows, 0, 4)
-    by_trade = by_trade + mm(dturn[:, head:], tval[head:, :])
+
+    @pl.when(inner == 0)
+    def _():
+        value(0, pair, 3, 4)
+        by_trades[...] = mm(dturn[:, :pair], tval[:pair, :])
+
+    @pl.when(inner == 1)
+    def _():
+        value(0, tail, 3, 4)
+        by_trades[...] = mm(dturn[:, :tail], tval[:tail, :])
+        arrive(*far_pass)
+        place(5)
+        value(tail, last, 0, 4)
+        by_trades[...] = by_trades[...] + mm(dturn[:, tail:], tval[tail:, :])
+
+    by_trade = by_trades[...]
     by_set = mm(jnp.concatenate(split3(by_trade), axis=0), table[...], NT)
     moments = (
         by_set[:REGRESSORS] + by_set[REGRESSORS : 2 * REGRESSORS] + by_set[2 * REGRESSORS :]
@@ -560,7 +630,7 @@
         dgrid[peers[trade_steps[s]]] = small[s, :REGRESSORS, :]
     for k in range(1, 4):
         for s in range(4):
-            dgrid[peers[trade_steps[s] + path_steps[k]]] = dall[k - 1, s]
+            dgrid[peers[trade_steps[s] + design_steps[k]]] = dall[k - 1, s]
     turned_all = jnp.concatenate([dgrid[i] for i in range(16)], axis=1)
     dstack[...] = jnp.concatenate(
         [turned_all, turned_all, turned_all, jnp.zeros_like(turned_all)], axis=0
@@ -574,13 +644,24 @@
 
     arrive(*moment_q)
     bzsend[...] = total(bq, 4)
-    pl.semaphore_wait(ready.at[4], 1)
+
+    @pl.when(inner == 0)
+    def _():
+        pl.semaphore_wait(ready.at[4], 1)
+
     moment_z = grouped(lambda peer: bzsend, bz.at[z], lines)
     start(*moment_z)
     fence()
     bz[z] = bzsend[...]
     work = eliminate(work, FIRST_STEPS, REGRESSORS)
     invert[...] = pltpu.roll(work, LANES - REGRESSORS, 1)
+    fence()
+    sigmoid(0, pair)
+
+    @pl.when(inner == 1)
+    def _():
+        sigmoid(pair, last)
+
     all_levels = tidx_ref[...]
     all_thresholds = jnp.zeros((4, quarter), F32)
     levels = tidx_ref[pl.ds(q, 1), :]
@@ -634,60 +715,100 @@
         [picked.astype(BF16), jnp.zeros((LANES - 3 * REGRESSORS, picked.shape[1]), BF16)], axis=0
     )
 
-    def slope(top, bottom):
-        spread = mm(dtri[top:bottom, :], solved3).astype(BF16).astype(F32)
-        slopes[top:bottom, :] = (nsig[top:bottom, :] * spread).astype(BF16)
+    def slope(top, bottom, left, right):
+        at = (slice(top, bottom), slice(left * trades, right * trades))
+        spread = mm(dtri[top:bottom, :], solved3[:, at[1]]).astype(BF16).astype(F32)
+        slopes[at] = (nsig[at] * spread).astype(BF16)
 
     scale = 1.0 / math.sqrt(paths_all)
 
-    def basis_part(first, last):
-        return mm(slopes[first * rows : last * rows, :], wall[...].reshape(4 * trades, feats))
-
-    def weight_part(left, right):
-        cut = slopes[:, left * trades : right * trades]
-        return mm(cut, pall[...], TN) * scale
-
-    slope(head, 4 * rows)
-    psend[0] = basis_part(3, 4).astype(BF16)
-    basis_via = pieces(psend.at[0], pvia, CORE, rows)
-    start(*basis_via)
+    def basis_part(first, final):
+        return mm(slopes[first * rows : final * rows, :], wall[...].reshape(4 * trades, feats))
+
+    def weight_part(left, right, depth):
+        cut = slopes[:depth, left * trades : right * trades]
+        return mm(cut, pall[:depth, :], TN) * scale
+
+    basis_via = [pieces(psend.at[i], pvia.at[i], CORE, rows, inner_copies) for i in range(2)]
+    basis_core = remote(psend.at[2], pq.at[0], CORE)
+    basis_far = pieces(pjoin.at[0], pq.at[1], FAR, rows, inner_copies)
+    basis_mid = pieces(pjoin.at[1], pq.at[1], MID, rows, inner_copies)
+    weight_via = pieces(wsend.at[0], wvia, SIDE, trades)
+    weight_side = remote(wsend.at[1], wz.at[0], SIDE)
+
+    def give(i, slot, depth, *group):
+        wsend[i] = weight_part(slot, slot + 1, depth).astype(BF16)
+        start(*group)
+        fence()
+
+    def join(i, onwards):
+        for p, (copy, onward) in enumerate(zip(basis_via[i], onwards)):
+            cut = slice(p * rows // PIECES, (p + 1) * rows // PIECES)
+            arrive(copy)
+            pjoin[i, cut, :] = (pown[i, cut, :] + pvia[i, cut, :].astype(F32)).astype(BF16)
+            start(onward)
+            fence()
+
+    def pull(depth):
+        pulled = mm(solved3, tval[:depth, :], NT)
+        pulls[:, :depth] = (
+            pulled[:REGRESSORS]
+            + pulled[REGRESSORS : 2 * REGRESSORS]
+            + pulled[2 * REGRESSORS : 3 * REGRESSORS]
+        )
+
+    @pl.when(inner == 1)
+    def _():
+        slope(0, last, 3, 4)
+        give(0, 3, last, *weight_via)
+        slope(head, last, 0, 3)
+        part = basis_part(4, 6)
+        psend[0] = part[rows:].astype(BF16)
+        start(*basis_via[0])
+        fence()
+        pown[0] = part[:rows]
+        slope(0, head, 0, 3)
+        psend[1] = basis_part(3, 4).astype(BF16)
+        start(*basis_via[1])
+        fence()
+        give(1, 2, last, weight_side)
+        join(0, basis_far)
+        part = basis_part(1, 3)
+        pown[1] = part[rows:]
+        join(1, basis_mid)
+        psend[2] = part[:rows].astype(BF16)
+        start(basis_core)
+        fence()
+        wnear[...] = weight_part(1, 2, last)
+        pull(last)
+
+    @pl.when(inner == 0)
+    def _():
+        slope(0, pair, 3, 4)
+        give(0, 3, pair, *weight_via)
+        slope(0, pair, 0, 3)
+        give(1, 2, pair, weight_side)
+        psend[2] = basis_part(1, 2).astype(BF16)
+        start(basis_core)
+        fence()
+        wnear[...] = weight_part(1, 2, pair)
+        pull(pair)
+
+    pull_via = [remote(esend.at[i], evia.at[i], CORE, inner_copies) for i in range(2)]
+    pull_core = remote(esend.at[2], eq.at[0], CORE)
+    pull_far = remote(ejoin.at[0], eq.at[1], FAR, inner_copies)
+    pull_mid = remote(ejoin.at[1], eq.at[1], MID, inner_copies)
+    esend[2] = pulls[:, rows:pair]
+    start(pull_core)
     fence()
-    slope(0, head)
-    part = weight_part(2, 4)
-    wsend[0] = part[trades:].astype(BF16)
-    weight_via = pieces(wsend.at[0], wvia, SIDE, trades)
-    start(*weight_via)
-    wsend[1] = part[:trades].astype(BF16)
-    weight_side = remote(wsend.at[1], wz.at[0], SIDE)
-    start(weight_side)
-    fence()
-    part = basis_part(1, 3)
-    pfar[...] = part[rows:]
-    basis_far = pieces(pjoin, pq.at[1], FAR, rows)
-    for p, (copy, onward) in enumerate(zip(basis_via, basis_far)):
-        cut = slice(p * rows // PIECES, (p + 1) * rows // PIECES)
-        arrive(copy)
-        pjoin[cut, :] = (pfar[cut, :] + pvia[cut, :].astype(F32)).astype(BF16)
-        start(onward)
+
+    @pl.when(inner == 1)
+    def _():
+        esend[0] = pulls[:, tail:]
+        esend[1] = pulls[:, 3 * rows : head]
+        start(*pull_via)
         fence()
-    psend[1] = part[:rows].astype(BF16)
-    basis_core = remote(psend.at[1], pq.at[0], CORE)
-    start(basis_core)
-    fence()
-    wnear[...] = weight_part(1, 2)
-    pulled = mm(solved3, tval[...], NT)
-    pulled = (
-        pulled[:REGRESSORS]
-        + pulled[REGRESSORS : 2 * REGRESSORS]
-        + pulled[2 * REGRESSORS : 3 * REGRESSORS]
-    )
-    esend[0] = pulled[:, 3 * rows :]
-    esend[1] = pulled[:, rows : 2 * rows]
-    pull_via = remote(esend.at[0], evia, CORE)
-    pull_core = remote(esend.at[1], eq.at[0], CORE)
-    pull_far = remote(ejoin, eq.at[1], FAR)
-    start(pull_via, pull_core)
-    fence()
+
     weight_near = pieces(wjoin, wz.at[1], NEAR, trades)
     for p, (copy, onward) in enumerate(zip(weight_via, weight_near)):
         cut = slice(p * trades // PIECES, (p + 1) * trades // PIECES)
@@ -695,11 +816,24 @@
         wjoin[cut, :] = (wnear[cut, :] + wvia[cut, :].astype(F32)).astype(BF16)
         start(onward)
         if p == 0:
-            arrive(pull_via)
-            ejoin[...] = pulled[:, 2 * rows : 3 * rows] + evia[...]
-            start(pull_far)
+
+            @pl.when(inner == 1)
+            def _():
+                arrive(*pull_via)
+                ejoin[0] = pulls[:, head:tail] + evia[0]
+                ejoin[1] = pulls[:, pair : 3 * rows] + evia[1]
+                start(pull_far, pull_mid)
+
     fence()
-    wadj_ref[...] = weight_part(0, 1)
+
+    @pl.when(inner == 1)
+    def _():
+        wadj_ref[...] = weight_part(0, 1, last)
+
+    @pl.when(inner == 0)
+    def _():
+        wadj_ref[...] = weight_part(0, 1, pair)
+
     basis_ref[...] = basis_part(0, 1)
 
     arrive(*coeffs_q)
@@ -711,7 +845,7 @@
     own_seed = full_rates * (jnp.where(over >= 0.0, 1.0, fall) / (1.0 + fall))
     residual = own_seed - mm(own_triple, stack3(solved_all))
     term = precise(coeffs_all, residual, NT) - precise(solved_all, fitted, NT)
-    term = term + pulled[:, :rows]
+    term = term + pulls[:, :rows]
     arrive(*loss_q)
     answers = jnp.concatenate([lq[i] for i in range(4)], axis=1)
     loss_sum = jnp.sum(answers[:1], axis=1, keepdims=True) / quarter
@@ -720,9 +854,26 @@
     basis_ref[...] = basis_ref[...] + pq[0].astype(F32)
     arrive(weight_side)
     wadj_ref[...] = wadj_ref[...] + wz[0].astype(F32)
-    arrive(*basis_far)
+
+    @pl.when(inner == 1)
+    def _():
+        arrive(*basis_mid)
+
+    @pl.when(inner == 0)
+    def _():
+        arrive(*basis_far)
+
     basis_ref[...] = basis_ref[...] + pq[1].astype(F32)
-    arrive(pull_core, pull_far)
+    arrive(pull_core)
+
+    @pl.when(inner == 1)
+    def _():
+        arrive(pull_mid)
+
+    @pl.when(inner == 0)
+    def _():
+        arrive(pull_far)
+
     term = term + eq[0] + eq[1]
     padded = jnp.concatenate([term, jnp.zeros((LANES - REGRESSORS, rows), F32)], axis=0)
     turned = pltpu.roll(jnp.transpose(padded), LANES - 1, 1)
@@ -736,18 +887,28 @@
     for copy in copies:
         copy.wait_send()
 
+    @pl.when(inner == 1)
+    def _():
+        for copy in inner_copies:
+            copy.wait_send()
+
+    @pl.when(inner == 0)
+    def _():
+        for copy in outer_copies:
+            copy.wait_send()
+
 
 def square_scratch(rows, trades, feats, set_total):
     size, quarter = REGRESSORS, set_total // 4
     return [
-        pltpu.VMEM((4 * rows, feats), BF16),
+        pltpu.VMEM((6 * rows, feats), BF16),
         pltpu.VMEM((4, trades, feats), BF16),
         pltpu.VMEM((4, size + 16, trades), BF16),
         pltpu.VMEM((3, 4, size, rows), BF16),
         pltpu.VMEM((16, size, rows), BF16),
         pltpu.VMEM((LANES, 16 * rows), BF16),
-        pltpu.VMEM((4 * rows, LANES), BF16),
-        pltpu.VMEM((size, 4 * rows), BF16),
+        pltpu.VMEM((6 * rows, LANES), BF16),
+        pltpu.VMEM((size, 6 * rows), BF16),
         pltpu.VMEM((set_total, 4 * trades), BF16),
         pltpu.VMEM((size, LANES), F32),
         pltpu.VMEM((4, size, quarter), F32),
@@ -761,27 +922,29 @@
         pltpu.VMEM((8, quarter), F32),
         pltpu.VMEM((4, 8, quarter), F32),
         pltpu.VMEM((quarter, 16 * rows), F32),
-        pltpu.VMEM((4 * rows, 4 * trades), BF16),
-        pltpu.VMEM((4 * rows, 4 * trades), F32),
-        pltpu.VMEM((4 * rows, 4 * trades), BF16),
+        pltpu.VMEM((size, 4 * trades), F32),
+        pltpu.VMEM((6 * rows, 4 * trades), BF16),
+        pltpu.VMEM((6 * rows, 4 * trades), F32),
+        pltpu.VMEM((6 * rows, 4 * trades), BF16),
+        pltpu.VMEM((size, 6 * rows), F32),
         pltpu.VMEM((2, trades, feats), BF16),
         pltpu.VMEM((trades, feats), BF16),
         pltpu.VMEM((trades, feats), F32),
         pltpu.VMEM((trades, feats), BF16),
         pltpu.VMEM((2, trades, feats), BF16),
+        pltpu.VMEM((3, rows, feats), BF16),
         pltpu.VMEM((2, rows, feats), BF16),
-        pltpu.VMEM((rows, feats), BF16),
-        pltpu.VMEM((rows, feats), F32),
-        pltpu.VMEM((rows, feats), BF16),
+        pltpu.VMEM((2, rows, feats), F32),
         pltpu.VMEM((2, rows, feats), BF16),
+        pltpu.VMEM((2, rows, feats), BF16),
+        pltpu.VMEM((3, size, rows), F32),
         pltpu.VMEM((2, size, rows), F32),
-        pltpu.VMEM((size, rows), F32),
-        pltpu.VMEM((size, rows), F32),
+        pltpu.VMEM((2, size, rows), F32),
         pltpu.VMEM((2, size, rows), F32),
         pltpu.SemaphoreType.DMA((7,)),
         pltpu.SemaphoreType.DMA((COPIES,)),
         pltpu.SemaphoreType.DMA((COPIES,)),
-        pltpu.SemaphoreType.REGULAR((5,)),
+        pltpu.SemaphoreType.REGULAR((6,)),
         pltpu.SemaphoreType.REGULAR,
     ]
 

time: 42.5 us -> 41.9 us (0.986)
  Pallas kernels: 39.2 us -> 38.6 us
    pallas_call x1, Pallas kernels: 39.2 us -> 38.6 us  [shards(): pl.pallas_call(body, out_shape=(jax.ShapeDtypeStruct((1, LANES), F32), ja...]
where the time goes in v3:
time: 41.9 us; the launch traced here: 41.8 us
  Pallas kernels  38.6 us (92%)
  between operations  1.8 us (4%)
  local copies, waits for them, and re-layouts  1.41 us (3%)
    pallas_call x1, Pallas kernels, shards(): pl.pallas_call(body, out_shape=(jax.ShapeDtypeStruct((1, LANES), F32), ja...  38.6 us
    unnamed x2, local copies, waits for them, and re-layouts  1.41 us

profile of v3, /device:TPU:0, one launch (start us, length us, event | category | flops | bytes accessed | tf_op | source)
XLA Modules:
  0.0 41.8 jit_solution(2619009454057836854)
XLA Ops:
  0.6 38.6 %shard_map.94 = (f32[1,128]{1,0:T(1,128)S(1)}, f32[128,512]{1,0:T(8,128)S(1)}, f32[128,512]{1,0:T(8,128)S(1)}) custom-call(bf16[128,512]{1,0:T(8,128)(2,1)} %pb_hbm.1, bf16[128,512]{1,0:T(8,128)(2,1)} %w_hbm.1, bf16[1,128]{1,0:T(2,128)(2,1)} %bitcast.10, s32[16,128]{1,0:T(8,128)} %bitcast.7, s32[4,128]{1,0:T(4,128)} %bitcast.8, f32[16]{0:T(128)} %level_hbm.1, ...), custom_call_target="tpu_custom_call" | custom-call | tf_op jit(solution)/shard_map/pallas_call | solution.py:1007
  39.2 0.7 %copy.14 = f32[128,512]{1,0:T(8,128)} copy(f32[128,512]{1,0:T(8,128)S(1)} %get-tuple-element.13) | data formatting | bytes 524288
  39.9 0.7 %copy.15 = f32[128,512]{1,0:T(8,128)} copy(f32[128,512]{1,0:T(8,128)S(1)} %get-tuple-element.14) | data formatting | bytes 524288

commit v4 on v3

--- a/solution.py
+++ b/solution.py
@@ -13,8 +13,8 @@
 PRECISE = lax.Precision.HIGHEST
 LANES = 128
 PIECES = 4
-FIRST_STEPS = 10
-COPIES = 96
+SENDS = 19
+ARRIVALS = 28
 F32 = jnp.float32
 BF16 = jnp.bfloat16
 
@@ -339,6 +339,28 @@
     wadj_ref[...] = total(wz, outer)
     for copy in pending:
         copy.wait_send()
+
+
+def pair_inverse(gram):
+    work = augmented(gram)
+    row = lax.broadcasted_iota(jnp.int32, work.shape, 0)
+    for k in range(0, REGRESSORS, 2):
+        left = jnp.broadcast_to(work[:, k : k + 1], work.shape)
+        right = jnp.broadcast_to(work[:, k + 1 : k + 2], work.shape)
+        a, c = left[k : k + 1, :], left[k + 1 : k + 2, :]
+        b, d = right[k : k + 1, :], right[k + 1 : k + 2, :]
+        above, below = work[k : k + 1, :], work[k + 1 : k + 2, :]
+        factor = 1.0 / (a * d - b * c)
+        upper = (d * above - b * below) * factor
+        lower = (a * below - c * above) * factor
+        rest = work - left * upper - right * lower
+        work = jnp.where(row == k, upper, jnp.where(row == k + 1, lower, rest))
+    return pltpu.roll(work, LANES - REGRESSORS, 1)
+
+
+def split2(x):
+    hi = x.astype(BF16)
+    return hi, (x - hi.astype(F32)).astype(BF16)
 
 
 def square(
@@ -401,16 +423,19 @@
     for load in loads:
         load.start()
 
-    made, copies, inner_copies, outer_copies = [], [], [], []
-
-    def remote(source, target, step, bag=copies):
-        k = len(made)
-        copy = pltpu.make_async_remote_copy(
-            src_ref=source, dst_ref=target, send_sem=send.at[k], recv_sem=recv.at[k],
+    copies, inner_copies, outer_copies = [], [], []
+    free_send, free_recv = list(range(SENDS)), list(range(ARRIVALS))
+
+    def wire(source, target, step, s, r):
+        return pltpu.make_async_remote_copy(
+            src_ref=source, dst_ref=target, send_sem=send.at[s], recv_sem=recv.at[r],
             device_id={"paths": peers[step]}, device_id_type=pl.DeviceIdType.MESH,
         )
-        made.append(copy)
-        bag.append(copy)
+
+    def remote(source, target, step, bag=copies):
+        s, r = free_send.pop(0), free_recv.pop(0)
+        copy = wire(source, target, step, s, r)
+        bag.append((copy, s))
         return copy
 
     def slot(i):
@@ -424,17 +449,55 @@
         pl.semaphore_signal(order, inc=1)
         pl.semaphore_wait(order, 1)
 
+    def drain(*keep):
+        kept = [id(copy) for copy in keep]
+
+        def settle(bag):
+            for copy, s in bag:
+                if id(copy) not in kept:
+                    copy.wait_send()
+                    free_send.append(s)
+            bag[:] = [pair for pair in bag if id(pair[0]) in kept]
+
+        settle(copies)
+
+        @pl.when(inner == 1)
+        def _():
+            settle(inner_copies)
+
+        @pl.when(inner == 0)
+        def _():
+            settle(outer_copies)
+
     def arrive(*group):
         for copy in group:
             copy.wait_recv()
 
+    def cuts(extent):
+        part = extent // PIECES
+        return [pl.ds(p * part, part) for p in range(PIECES)]
+
     def pieces(source, target, step, extent, bag=copies):
-        part = extent // PIECES
-        cuts = [pl.ds(p * part, part) for p in range(PIECES)]
-        return [remote(source.at[cut], target.at[cut], step, bag) for cut in cuts]
-
-    def grouped(source, target, bits):
-        return [remote(source(peers[s]), target, s) for s in bits]
+        s = free_send.pop(0)
+        rs = [free_recv.pop(0) for _ in range(PIECES)]
+        bag.append((wire(source, target, step, s, rs[0]), s))
+        return [
+            wire(source.at[cut], target.at[cut], step, s, r) for cut, r in zip(cuts(extent), rs)
+        ]
+
+    def parcel(source, target, step, extent, bag=copies):
+        s, r = free_send.pop(0), free_recv.pop(0)
+        whole = wire(source, target, step, s, r)
+        bag.append((whole, s))
+        parts = [wire(source.at[cut], target.at[cut], step, s, r) for cut in cuts(extent)]
+        return parts, whole
+
+    def grouped(source, target, place, steps):
+        s, r = free_send.pop(0), free_recv.pop(0)
+        three = target.at[pl.ds(0, 3)]
+        whole = wire(three, three, steps[0], s, r)
+        copies.append((whole, s))
+        return [wire(source(peers[t]), target.at[place], t, s, r) for t in steps], whole
 
     def place(i):
         design = design_of(pall[i * rows : (i + 1) * rows, :])
@@ -445,7 +508,7 @@
         return turned
 
     path_core = remote(pb_hbm, slot(1), CORE)
-    trade_side = pieces(w_hbm, wall.at[2], SIDE, trades)
+    trade_side, side_all = parcel(w_hbm, wall.at[2], SIDE, trades)
     trade_near = pieces(w_hbm, wall.at[1], NEAR, trades)
     path_mid = pieces(pb_hbm, slot(2), MID, rows, inner_copies)
     path_far = pieces(pb_hbm, slot(4), FAR, rows, outer_copies)
@@ -516,9 +579,10 @@
 
     loads[2].wait()
     small_pass = remote(small.at[1], small.at[3], SIDE)
-    trade_pass = pieces(wall.at[1], wall.at[3], SIDE, trades)
-    mid_pass = pieces(slot(2), slot(3), CORE, rows, inner_copies)
-    far_pass = pieces(slot(4), slot(5), CORE, rows, inner_copies)
+    trade_pass, pass_all = parcel(wall.at[1], wall.at[3], SIDE, trades)
+    mid_pass, mid_all = parcel(slot(2), slot(3), CORE, rows, inner_copies)
+    far_pass, far_all = parcel(slot(4), slot(5), CORE, rows, inner_copies)
+    used = [r for r in range(ARRIVALS) if r not in free_recv]
     front = pl.ds(0, REGRESSORS)
     design_core = remote(small.at[:, front], dall.at[0], CORE)
     design_far = remote(small.at[:, front], dall.at[1], FAR)
@@ -565,13 +629,13 @@
             start(small_pass)
         arrive(copy)
         start(onward)
-    arrive(*trade_side, small_side)
+    arrive(side_all, small_side)
     value(0, pair, 0, 3)
 
     @pl.when(inner == 1)
     def _():
         place(2)
-        arrive(*mid_pass)
+        arrive(mid_all)
         place(3)
         value(pair, head, 0, 3)
         for copy, onward in zip(path_far, far_pass):
@@ -585,7 +649,7 @@
     arrive(small_pass)
     start(design_core, design_far)
     fence()
-    arrive(*trade_pass)
+    arrive(pass_all)
 
     @pl.when(inner == 0)
     def _():
@@ -596,7 +660,7 @@
     def _():
         value(0, tail, 3, 4)
         by_trades[...] = mm(dturn[:, :tail], tval[:tail, :])
-        arrive(*far_pass)
+        arrive(far_all)
         place(5)
         value(tail, last, 0, 4)
         by_trades[...] = by_trades[...] + mm(dturn[:, tail:], tval[tail:, :])
@@ -617,13 +681,32 @@
             result = result + ref[i].astype(F32)
         return result
 
-    moment_q = grouped(lambda peer: bown.at[lax.rem(peer, 4)], bq.at[q], quads)
+    moment_q, moment_all = grouped(lambda peer: bown.at[lax.rem(peer, 4)], bq, q, quads)
     start(*moment_q)
     fence()
     bq[q] = bown[q]
 
-    arrive(design_far)
-    start(design_pass)
+    @pl.when(inner == 1)
+    def _():
+        arrive(design_far)
+        start(design_pass)
+
+    arrive(moment_all)
+    bzsend[...] = total(bq, 4)
+
+    @pl.when(inner == 0)
+    def _():
+        pl.semaphore_wait(ready.at[4], 1)
+
+    moment_z, moment_all = grouped(lambda peer: bzsend, bz, z, lines)
+    start(*moment_z)
+    fence()
+    bz[z] = bzsend[...]
+    @pl.when(inner == 0)
+    def _():
+        arrive(design_far)
+        start(design_pass)
+
     fence()
     arrive(design_core, design_pass)
     for s in range(4):
@@ -640,21 +723,7 @@
     gram_row = lax.broadcasted_iota(jnp.int32, (REGRESSORS, LANES), 0)
     gram_lane = lax.broadcasted_iota(jnp.int32, (REGRESSORS, LANES), 1)
     ridge = jnp.where(gram_row == gram_lane, RIDGE_SCALE * paths_all, 0.0)
-    work = eliminate(augmented(gram + ridge), 0, FIRST_STEPS)
-
-    arrive(*moment_q)
-    bzsend[...] = total(bq, 4)
-
-    @pl.when(inner == 0)
-    def _():
-        pl.semaphore_wait(ready.at[4], 1)
-
-    moment_z = grouped(lambda peer: bzsend, bz.at[z], lines)
-    start(*moment_z)
-    fence()
-    bz[z] = bzsend[...]
-    work = eliminate(work, FIRST_STEPS, REGRESSORS)
-    invert[...] = pltpu.roll(work, LANES - REGRESSORS, 1)
+    invert[...] = pair_inverse(gram + ridge)
     fence()
     sigmoid(0, pair)
 
@@ -677,23 +746,21 @@
     full_thresholds = jnp.concatenate([all_thresholds[i : i + 1] for i in range(4)], axis=1)
     full_rates = jnp.concatenate([all_rates[i : i + 1] for i in range(4)], axis=1)
 
-    arrive(*moment_z)
+    arrive(moment_all)
     inverse = invert[:, :REGRESSORS]
     coeffs = precise(inverse, total(bz, 4))
     csend[...] = coeffs
-    coeffs_q = grouped(lambda peer: csend, cq.at[q], quads)
+    coeffs_q, coeffs_all_sent = grouped(lambda peer: csend, cq, q, quads)
     cq[q] = coeffs
     excess = mm(stack3(coeffs), dstack[...], TN) - thresholds
     over_ref[...] = excess
     fade = jnp.exp(-jnp.abs(excess))
     seed = rate * (jnp.where(excess >= 0.0, 1.0, fade) / (1.0 + fade))
-    seed_cut = mm(dstack[:REGRESSORS, :], jnp.concatenate(split3(seed), axis=0), NT)
-    seed_sum = (
-        seed_cut[:, :quarter] + seed_cut[:, quarter : 2 * quarter] + seed_cut[:, 2 * quarter :]
-    )
+    seed_cut = mm(dstack[:REGRESSORS, :], jnp.concatenate(split2(seed), axis=0), NT)
+    seed_sum = seed_cut[:, :quarter] + seed_cut[:, quarter:]
     solved = precise(inverse, seed_sum)
     ssend[...] = solved
-    answer_q = grouped(lambda peer: ssend, sq.at[q], quads)
+    answer_q, answer_all = grouped(lambda peer: ssend, sq, q, quads)
     start(*answer_q)
     start(*coeffs_q)
     fence()
@@ -704,11 +771,12 @@
     loss_part = jnp.sum(rate * jnp.sum(loss, axis=1, keepdims=True), axis=0, keepdims=True)
     lsend[...] = jnp.broadcast_to(loss_part, lsend.shape)
     lq[q] = lsend[...]
-    loss_q = grouped(lambda peer: lsend, lq.at[q], quads)
+    loss_q, loss_all = grouped(lambda peer: lsend, lq, q, quads)
     start(*loss_q)
     fence()
 
-    arrive(*answer_q)
+    drain(answer_all, coeffs_all_sent, loss_all)
+    arrive(answer_all)
     solved_all = jnp.concatenate([sq[i] for i in range(4)], axis=1)
     picked = mm(jnp.concatenate(split3(solved_all), axis=0), table[...])
     solved3 = jnp.concatenate(
@@ -729,10 +797,15 @@
         cut = slopes[:depth, left * trades : right * trades]
         return mm(cut, pall[:depth, :], TN) * scale
 
-    basis_via = [pieces(psend.at[i], pvia.at[i], CORE, rows, inner_copies) for i in range(2)]
+    free_recv.extend(used)
+    basis_via = [remote(psend.at[i], pvia.at[i], CORE, inner_copies) for i in range(2)]
     basis_core = remote(psend.at[2], pq.at[0], CORE)
-    basis_far = pieces(pjoin.at[0], pq.at[1], FAR, rows, inner_copies)
-    basis_mid = pieces(pjoin.at[1], pq.at[1], MID, rows, inner_copies)
+    basis_far = remote(pjoin.at[0], pq.at[1], FAR, inner_copies)
+    basis_mid = remote(pjoin.at[1], pq.at[1], MID, inner_copies)
+    pull_via = [remote(esend.at[i], evia.at[i], CORE, inner_copies) for i in range(2)]
+    pull_core = remote(esend.at[2], eq.at[0], CORE)
+    pull_far = remote(ejoin.at[0], eq.at[1], FAR, inner_copies)
+    pull_mid = remote(ejoin.at[1], eq.at[1], MID, inner_copies)
     weight_via = pieces(wsend.at[0], wvia, SIDE, trades)
     weight_side = remote(wsend.at[1], wz.at[0], SIDE)
 
@@ -741,13 +814,11 @@
         start(*group)
         fence()
 
-    def join(i, onwards):
-        for p, (copy, onward) in enumerate(zip(basis_via[i], onwards)):
-            cut = slice(p * rows // PIECES, (p + 1) * rows // PIECES)
-            arrive(copy)
-            pjoin[i, cut, :] = (pown[i, cut, :] + pvia[i, cut, :].astype(F32)).astype(BF16)
-            start(onward)
-            fence()
+    def join(i, onward):
+        arrive(basis_via[i])
+        pjoin[i] = (pown[i] + pvia[i].astype(F32)).astype(BF16)
+        start(onward)
+        fence()
 
     def pull(depth):
         pulled = mm(solved3, tval[:depth, :], NT)
@@ -764,23 +835,33 @@
         slope(head, last, 0, 3)
         part = basis_part(4, 6)
         psend[0] = part[rows:].astype(BF16)
-        start(*basis_via[0])
+        start(basis_via[0])
         fence()
         pown[0] = part[:rows]
         slope(0, head, 0, 3)
         psend[1] = basis_part(3, 4).astype(BF16)
-        start(*basis_via[1])
+        start(basis_via[1])
         fence()
         give(1, 2, last, weight_side)
         join(0, basis_far)
+        pull(last)
+        esend[0] = pulls[:, tail:]
+        esend[1] = pulls[:, 3 * rows : head]
+        esend[2] = pulls[:, rows:pair]
+        start(*pull_via, pull_core)
+        fence()
         part = basis_part(1, 3)
         pown[1] = part[rows:]
-        join(1, basis_mid)
         psend[2] = part[:rows].astype(BF16)
         start(basis_core)
         fence()
+        arrive(*pull_via)
+        ejoin[0] = pulls[:, head:tail] + evia[0]
+        ejoin[1] = pulls[:, pair : 3 * rows] + evia[1]
+        start(pull_far, pull_mid)
+        fence()
+        join(1, basis_mid)
         wnear[...] = weight_part(1, 2, last)
-        pull(last)
 
     @pl.when(inner == 0)
     def _():
@@ -793,36 +874,17 @@
         fence()
         wnear[...] = weight_part(1, 2, pair)
         pull(pair)
-
-    pull_via = [remote(esend.at[i], evia.at[i], CORE, inner_copies) for i in range(2)]
-    pull_core = remote(esend.at[2], eq.at[0], CORE)
-    pull_far = remote(ejoin.at[0], eq.at[1], FAR, inner_copies)
-    pull_mid = remote(ejoin.at[1], eq.at[1], MID, inner_copies)
-    esend[2] = pulls[:, rows:pair]
-    start(pull_core)
-    fence()
-
-    @pl.when(inner == 1)
-    def _():
-        esend[0] = pulls[:, tail:]
-        esend[1] = pulls[:, 3 * rows : head]
-        start(*pull_via)
+        esend[2] = pulls[:, rows:pair]
+        start(pull_core)
         fence()
 
     weight_near = pieces(wjoin, wz.at[1], NEAR, trades)
+    near_all = copies[-1][0]
     for p, (copy, onward) in enumerate(zip(weight_via, weight_near)):
         cut = slice(p * trades // PIECES, (p + 1) * trades // PIECES)
         arrive(copy)
         wjoin[cut, :] = (wnear[cut, :] + wvia[cut, :].astype(F32)).astype(BF16)
         start(onward)
-        if p == 0:
-
-            @pl.when(inner == 1)
-            def _():
-                arrive(*pull_via)
-                ejoin[0] = pulls[:, head:tail] + evia[0]
-                ejoin[1] = pulls[:, pair : 3 * rows] + evia[1]
-                start(pull_far, pull_mid)
 
     fence()
 
@@ -836,7 +898,7 @@
 
     basis_ref[...] = basis_part(0, 1)
 
-    arrive(*coeffs_q)
+    arrive(coeffs_all_sent)
     own_triple = dtri[:rows, :]
     coeffs_all = jnp.concatenate([cq[i] for i in range(4)], axis=1)
     fitted = mm(own_triple, stack3(coeffs_all))
@@ -846,7 +908,7 @@
     residual = own_seed - mm(own_triple, stack3(solved_all))
     term = precise(coeffs_all, residual, NT) - precise(solved_all, fitted, NT)
     term = term + pulls[:, :rows]
-    arrive(*loss_q)
+    arrive(loss_all)
     answers = jnp.concatenate([lq[i] for i in range(4)], axis=1)
     loss_sum = jnp.sum(answers[:1], axis=1, keepdims=True) / quarter
     loss_ref[...] = jnp.broadcast_to(loss_sum / (paths_all * set_total), loss_ref.shape)
@@ -857,13 +919,14 @@
 
     @pl.when(inner == 1)
     def _():
-        arrive(*basis_mid)
+        arrive(basis_mid)
 
     @pl.when(inner == 0)
     def _():
-        arrive(*basis_far)
+        arrive(basis_far)
 
     basis_ref[...] = basis_ref[...] + pq[1].astype(F32)
+    drain(near_all, basis_mid, pull_far, pull_mid)
     arrive(pull_core)
 
     @pl.when(inner == 1)
@@ -884,18 +947,7 @@
         cut = slice(p * trades // PIECES, (p + 1) * trades // PIECES)
         arrive(copy)
         wadj_ref[cut, :] = wadj_ref[cut, :] + wz[1, cut, :].astype(F32)
-    for copy in copies:
-        copy.wait_send()
-
-    @pl.when(inner == 1)
-    def _():
-        for copy in inner_copies:
-            copy.wait_send()
-
-    @pl.when(inner == 0)
-    def _():
-        for copy in outer_copies:
-            copy.wait_send()
+    drain()
 
 
 def square_scratch(rows, trades, feats, set_total):
@@ -942,8 +994,8 @@
         pltpu.VMEM((2, size, rows), F32),
         pltpu.VMEM((2, size, rows), F32),
         pltpu.SemaphoreType.DMA((7,)),
-        pltpu.SemaphoreType.DMA((COPIES,)),
-        pltpu.SemaphoreType.DMA((COPIES,)),
+        pltpu.SemaphoreType.DMA((SENDS,)),
+        pltpu.SemaphoreType.DMA((ARRIVALS,)),
         pltpu.SemaphoreType.REGULAR((6,)),
         pltpu.SemaphoreType.REGULAR,
     ]

time: 41.9 us -> 40.2 us (0.959)
  Pallas kernels: 38.6 us -> 36.9 us
    pallas_call x1, Pallas kernels: 38.6 us -> 36.9 us  [shards(): pl.pallas_call(body, out_shape=(jax.ShapeDtypeStruct((1, LANES), F32), ja...]
where the time goes in v4:
time: 40.2 us; the launch traced here: 40.1 us
  Pallas kernels  36.9 us (92%)
  between operations  1.8 us (4%)
  local copies, waits for them, and re-layouts  1.41 us (4%)
    pallas_call x1, Pallas kernels, shards(): pl.pallas_call(body, out_shape=(jax.ShapeDtypeStruct((1, LANES), F32), ja...  36.9 us
    unnamed x2, local copies, waits for them, and re-layouts  1.41 us

profile of v4, /device:TPU:0, one launch (start us, length us, event | category | flops | bytes accessed | tf_op | source)
XLA Modules:
  0.0 40.1 jit_solution(2373082850909402714)
XLA Ops:
  0.6 36.9 %shard_map.94 = (f32[1,128]{1,0:T(1,128)S(1)}, f32[128,512]{1,0:T(8,128)S(1)}, f32[128,512]{1,0:T(8,128)S(1)}) custom-call(bf16[128,512]{1,0:T(8,128)(2,1)} %pb_hbm.1, bf16[128,512]{1,0:T(8,128)(2,1)} %w_hbm.1, bf16[1,128]{1,0:T(2,128)(2,1)} %bitcast.10, s32[16,128]{1,0:T(8,128)} %bitcast.7, s32[4,128]{1,0:T(4,128)} %bitcast.8, f32[16]{0:T(128)} %level_hbm.1, ...), custom_call_target="tpu_custom_call" | custom-call | tf_op jit(solution)/shard_map/pallas_call | solution.py:1059
  37.5 0.7 %copy.14 = f32[128,512]{1,0:T(8,128)} copy(f32[128,512]{1,0:T(8,128)S(1)} %get-tuple-element.13) | data formatting | bytes 524288
  38.3 0.7 %copy.15 = f32[128,512]{1,0:T(8,128)} copy(f32[128,512]{1,0:T(8,128)S(1)} %get-tuple-element.14) | data formatting | bytes 524288

commit v5 on v4

--- a/solution.py
+++ b/solution.py
@@ -649,21 +649,21 @@
     arrive(small_pass)
     start(design_core, design_far)
     fence()
-    arrive(pass_all)
 
     @pl.when(inner == 0)
     def _():
+        arrive(pass_all)
         value(0, pair, 3, 4)
         by_trades[...] = mm(dturn[:, :pair], tval[:pair, :])
 
     @pl.when(inner == 1)
     def _():
-        value(0, tail, 3, 4)
-        by_trades[...] = mm(dturn[:, :tail], tval[:tail, :])
         arrive(far_all)
         place(5)
-        value(tail, last, 0, 4)
-        by_trades[...] = by_trades[...] + mm(dturn[:, tail:], tval[tail:, :])
+        value(tail, last, 0, 3)
+        arrive(pass_all)
+        value(0, last, 3, 4)
+        by_trades[...] = mm(dturn[...], tval[...])
 
     by_trade = by_trades[...]
     by_set = mm(jnp.concatenate(split3(by_trade), axis=0), table[...], NT)
@@ -755,9 +755,9 @@
     excess = mm(stack3(coeffs), dstack[...], TN) - thresholds
     over_ref[...] = excess
     fade = jnp.exp(-jnp.abs(excess))
-    seed = rate * (jnp.where(excess >= 0.0, 1.0, fade) / (1.0 + fade))
+    seed = jnp.where(excess >= 0.0, 1.0, fade) / (1.0 + fade)
     seed_cut = mm(dstack[:REGRESSORS, :], jnp.concatenate(split2(seed), axis=0), NT)
-    seed_sum = seed_cut[:, :quarter] + seed_cut[:, quarter:]
+    seed_sum = (seed_cut[:, :quarter] + seed_cut[:, quarter:]) * rate_ref[pl.ds(q, 1), :]
     solved = precise(inverse, seed_sum)
     ssend[...] = solved
     answer_q, answer_all = grouped(lambda peer: ssend, sq, q, quads)
@@ -830,20 +830,20 @@
 
     @pl.when(inner == 1)
     def _():
-        slope(0, last, 3, 4)
-        give(0, 3, last, *weight_via)
-        slope(head, last, 0, 3)
+        slope(head, last, 0, 4)
         part = basis_part(4, 6)
         psend[0] = part[rows:].astype(BF16)
         start(basis_via[0])
         fence()
         pown[0] = part[:rows]
+        slope(0, head, 3, 4)
+        give(0, 3, last, *weight_via)
         slope(0, head, 0, 3)
         psend[1] = basis_part(3, 4).astype(BF16)
         start(basis_via[1])
         fence()
+        join(0, basis_far)
         give(1, 2, last, weight_side)
-        join(0, basis_far)
         pull(last)
         esend[0] = pulls[:, tail:]
         esend[1] = pulls[:, 3 * rows : head]
@@ -1037,6 +1037,18 @@
         pltpu.SemaphoreType.DMA((7, q_pairs)),
         pltpu.SemaphoreType.DMA((7, q_pairs)),
     ]
+
+
+def publish(*refs):
+    sources, targets, done = refs[:3], refs[3:6], refs[6]
+    copies = [
+        pltpu.make_async_copy(source, target, done.at[i])
+        for i, (source, target) in enumerate(zip(sources, targets))
+    ]
+    for copy in copies:
+        copy.start()
+    for copy in copies:
+        copy.wait()
 
 
 def shards(
@@ -1090,6 +1102,15 @@
             )
         )
     )
+    results = (loss, basis_adjoint, weight_adjoint)
+    loss, basis_adjoint, weight_adjoint = pl.pallas_call(
+        publish,
+        out_shape=[jax.ShapeDtypeStruct(result.shape, result.dtype) for result in results],
+        in_specs=[pl.BlockSpec(memory_space=pl.ANY)] * 3,
+        out_specs=[pl.BlockSpec(memory_space=pl.ANY)] * 3,
+        scratch_shapes=[pltpu.SemaphoreType.DMA((3,))],
+        compiler_params=pltpu.CompilerParams(vmem_limit_bytes=1024 * 1024),
+    )(*results)
     return loss[0, :1], basis_adjoint, weight_adjoint
 
 

time: 40.2 us -> 37.6 us (0.935)
  local copies, waits for them, and re-layouts: 1.41 us -> 0 us
  between operations: 1.8 us -> 0.64 us
    unnamed x2 -> x0, local copies, waits for them, and re-layouts: 1.41 us -> none
    pallas_call x1, Pallas kernels: 36.9 us -> 36 us  [shards(): pl.pallas_call(body, out_shape=(jax.ShapeDtypeStruct((1, LANES), F32), ja...]
    pallas_call x0 -> x1, Pallas kernels: none -> 0.82 us  [shards(): pl.pallas_call(publish, out_shape=[jax.ShapeDtypeStruct(result.shape, res...]
where the time goes in v5:
time: 37.6 us; the launch traced here: 37.5 us
  Pallas kernels  36.8 us (98%)
  between operations  0.64 us (2%)
    pallas_call x1, Pallas kernels, shards(): pl.pallas_call(body, out_shape=(jax.ShapeDtypeStruct((1, LANES), F32), ja...  36 us
    pallas_call x1, Pallas kernels, shards(): pl.pallas_call(publish, out_shape=[jax.ShapeDtypeStruct(result.shape, res...  0.82 us

profile of v5, /device:TPU:0, one launch (start us, length us, event | category | flops | bytes accessed | tf_op | source)
XLA Modules:
  0.0 37.5 jit_solution(15305028224893845375)
XLA Ops:
  0.6 36.0 %shard_map.94 = (f32[1,128]{1,0:T(1,128)S(1)}, f32[128,512]{1,0:T(8,128)S(1)}, f32[128,512]{1,0:T(8,128)S(1)}) custom-call(bf16[128,512]{1,0:T(8,128)(2,1)} %pb_hbm.1, bf16[128,512]{1,0:T(8,128)(2,1)} %w_hbm.1, bf16[1,128]{1,0:T(2,128)(2,1)} %bitcast.9, s32[16,128]{1,0:T(8,128)} %bitcast.6, s32[4,128]{1,0:T(4,128)} %bitcast.7, f32[16]{0:T(128)} %level_hbm.1, ...), custom_call_target="tpu_custom_call" | custom-call | tf_op jit(solution)/shard_map/pallas_call | solution.py:1071
  36.6 0.8 %shard_map.95 = (f32[1,128]{1,0:T(1,128)}, f32[128,512]{1,0:T(8,128)}, f32[128,512]{1,0:T(8,128)}) custom-call(f32[1,128]{1,0:T(1,128)S(1)} %get-tuple-element.9.refs_0_, f32[128,512]{1,0:T(8,128)S(1)} %get-tuple-element.10.refs_1_, f32[128,512]{1,0:T(8,128)S(1)} %get-tuple-element.11.refs_2_), custom_call_target="tpu_custom_call" | custom-call | tf_op jit(solution)/shard_map/pallas_call | solution.py:1106

commit v6 on v5

--- a/solution.py
+++ b/solution.py
@@ -617,18 +617,18 @@
     arrive(path_core)
     place(1)
 
-    @pl.when(inner == 1)
-    def _():
-        for copy, onward in zip(path_mid, mid_pass):
-            arrive(copy)
-            start(onward)
-
     for p, (copy, onward) in enumerate(zip(trade_near, trade_pass)):
         if p == split:
             arrive(small_near)
             start(small_pass)
         arrive(copy)
         start(onward)
+    @pl.when(inner == 1)
+    def _():
+        for copy, onward in zip(path_mid, mid_pass):
+            arrive(copy)
+            start(onward)
+
     arrive(side_all, small_side)
     value(0, pair, 0, 3)
 

time: 37.6 us -> 36.7 us (0.976)
  Pallas kernels: 36.8 us -> 35.9 us
    pallas_call x1, Pallas kernels: 36 us -> 35.1 us  [shards(): pl.pallas_call(body, out_shape=(jax.ShapeDtypeStruct((1, LANES), F32), ja...]
where the time goes in v6:
time: 36.7 us; the launch traced here: 36.5 us
  Pallas kernels  35.9 us (98%)
  between operations  0.64 us (2%)
    pallas_call x1, Pallas kernels, shards(): pl.pallas_call(body, out_shape=(jax.ShapeDtypeStruct((1, LANES), F32), ja...  35.1 us
    pallas_call x1, Pallas kernels, shards(): pl.pallas_call(publish, out_shape=[jax.ShapeDtypeStruct(result.shape, res...  0.82 us

profile of v6, /device:TPU:0, one launch (start us, length us, event | category | flops | bytes accessed | tf_op | source)
XLA Modules:
  0.0 36.5 jit_solution(10474734839908497301)
XLA Ops:
  0.6 35.1 %shard_map.94 = (f32[1,128]{1,0:T(1,128)S(1)}, f32[128,512]{1,0:T(8,128)S(1)}, f32[128,512]{1,0:T(8,128)S(1)}) custom-call(bf16[128,512]{1,0:T(8,128)(2,1)} %pb_hbm.1, bf16[128,512]{1,0:T(8,128)(2,1)} %w_hbm.1, bf16[1,128]{1,0:T(2,128)(2,1)} %bitcast.9, s32[16,128]{1,0:T(8,128)} %bitcast.6, s32[4,128]{1,0:T(4,128)} %bitcast.7, f32[16]{0:T(128)} %level_hbm.1, ...), custom_call_target="tpu_custom_call" | custom-call | tf_op jit(solution)/shard_map/pallas_call | solution.py:1071
  35.7 0.8 %shard_map.95 = (f32[1,128]{1,0:T(1,128)}, f32[128,512]{1,0:T(8,128)}, f32[128,512]{1,0:T(8,128)}) custom-call(f32[1,128]{1,0:T(1,128)S(1)} %get-tuple-element.9.refs_0_, f32[128,512]{1,0:T(8,128)S(1)} %get-tuple-element.10.refs_1_, f32[128,512]{1,0:T(8,128)S(1)} %get-tuple-element.11.refs_2_), custom_call_target="tpu_custom_call" | custom-call | tf_op jit(solution)/shard_map/pallas_call | solution.py:1106

commit v7 on v6

--- a/solution.py
+++ b/solution.py
@@ -370,7 +370,7 @@
     not_ref, set_ref, tidx_ref, level_ref, rate_ref,
     pall, wall, small, dall, dgrid, dstack, dtri, dturn, table, invert,
     bown, bq, bzsend, bz, csend, cq, ssend, sq, lsend, lq, over_ref,
-    by_trades, tval, nsig, slopes, pulls,
+    partial, tval, nsig, slopes, pulls,
     wsend, wvia, wnear, wjoin, wz, psend, pvia, pown, pjoin, pq, esend, evia, ejoin, eq,
     local, send, recv, ready, order,
 ):
@@ -650,26 +650,32 @@
     start(design_core, design_far)
     fence()
 
+    def gather(depth, left, right):
+        at = slice(left * trades, right * trades)
+        by_trade = mm(dturn[:, :depth], tval[:depth, at])
+        by_set = mm(jnp.concatenate(split3(by_trade), axis=0), table[:, at], NT)
+        return (
+            by_set[:REGRESSORS] + by_set[REGRESSORS : 2 * REGRESSORS] + by_set[2 * REGRESSORS :]
+        )
+
     @pl.when(inner == 0)
     def _():
+        partial[...] = gather(pair, 0, 3)
         arrive(pass_all)
         value(0, pair, 3, 4)
-        by_trades[...] = mm(dturn[:, :pair], tval[:pair, :])
+        partial[...] = partial[...] + gather(pair, 3, 4)
 
     @pl.when(inner == 1)
     def _():
         arrive(far_all)
         place(5)
         value(tail, last, 0, 3)
+        partial[...] = gather(last, 0, 3)
         arrive(pass_all)
         value(0, last, 3, 4)
-        by_trades[...] = mm(dturn[...], tval[...])
-
-    by_trade = by_trades[...]
-    by_set = mm(jnp.concatenate(split3(by_trade), axis=0), table[...], NT)
-    moments = (
-        by_set[:REGRESSORS] + by_set[REGRESSORS : 2 * REGRESSORS] + by_set[2 * REGRESSORS :]
-    )
+        partial[...] = partial[...] + gather(last, 3, 4)
+
+    moments = partial[...]
     for i in range(4):
         bown[i] = moments[:, i * quarter : (i + 1) * quarter]
     quads = (CORE + SIDE, SIDE, CORE)
@@ -974,7 +980,7 @@
         pltpu.VMEM((8, quarter), F32),
         pltpu.VMEM((4, 8, quarter), F32),
         pltpu.VMEM((quarter, 16 * rows), F32),
-        pltpu.VMEM((size, 4 * trades), F32),
+        pltpu.VMEM((size, set_total), F32),
         pltpu.VMEM((6 * rows, 4 * trades), BF16),
         pltpu.VMEM((6 * rows, 4 * trades), F32),
         pltpu.VMEM((6 * rows, 4 * trades), BF16),

time: 36.7 us -> 36.4 us (level)
  no operation moved by 1% of the time
where the time goes in v7:
time: 36.4 us; the launch traced here: 36.2 us
  Pallas kernels  35.6 us (98%)
  between operations  0.64 us (2%)
    pallas_call x1, Pallas kernels, shards(): pl.pallas_call(body, out_shape=(jax.ShapeDtypeStruct((1, LANES), F32), ja...  34.8 us
    pallas_call x1, Pallas kernels, shards(): pl.pallas_call(publish, out_shape=[jax.ShapeDtypeStruct(result.shape, res...  0.82 us

profile of v7, /device:TPU:0, one launch (start us, length us, event | category | flops | bytes accessed | tf_op | source)
XLA Modules:
  0.0 36.2 jit_solution(4972027144526351238)
XLA Ops:
  0.6 34.8 %shard_map.94 = (f32[1,128]{1,0:T(1,128)S(1)}, f32[128,512]{1,0:T(8,128)S(1)}, f32[128,512]{1,0:T(8,128)S(1)}) custom-call(bf16[128,512]{1,0:T(8,128)(2,1)} %pb_hbm.1, bf16[128,512]{1,0:T(8,128)(2,1)} %w_hbm.1, bf16[1,128]{1,0:T(2,128)(2,1)} %bitcast.9, s32[16,128]{1,0:T(8,128)} %bitcast.6, s32[4,128]{1,0:T(4,128)} %bitcast.7, f32[16]{0:T(128)} %level_hbm.1, ...), custom_call_target="tpu_custom_call" | custom-call | tf_op jit(solution)/shard_map/pallas_call | solution.py:1077
  35.4 0.8 %shard_map.95 = (f32[1,128]{1,0:T(1,128)}, f32[128,512]{1,0:T(8,128)}, f32[128,512]{1,0:T(8,128)}) custom-call(f32[1,128]{1,0:T(1,128)S(1)} %get-tuple-element.9.refs_0_, f32[128,512]{1,0:T(8,128)S(1)} %get-tuple-element.10.refs_1_, f32[128,512]{1,0:T(8,128)S(1)} %get-tuple-element.11.refs_2_), custom_call_target="tpu_custom_call" | custom-call | tf_op jit(solution)/shard_map/pallas_call | solution.py:1112

commit v8 on v7

--- a/solution.py
+++ b/solution.py
@@ -836,12 +836,12 @@
 
     @pl.when(inner == 1)
     def _():
-        slope(head, last, 0, 4)
-        part = basis_part(4, 6)
-        psend[0] = part[rows:].astype(BF16)
+        slope(tail, last, 0, 4)
+        psend[0] = basis_part(5, 6).astype(BF16)
         start(basis_via[0])
         fence()
-        pown[0] = part[:rows]
+        slope(head, tail, 0, 4)
+        pown[0] = basis_part(4, 5)
         slope(0, head, 3, 4)
         give(0, 3, last, *weight_via)
         slope(0, head, 0, 3)

time: 36.4 us -> 36.4 us (level)
  no operation moved by 1% of the time
where the time goes in v8:
time: 36.4 us; the launch traced here: 36.2 us
  Pallas kernels  35.6 us (98%)
  between operations  0.64 us (2%)
    pallas_call x1, Pallas kernels, shards(): pl.pallas_call(body, out_shape=(jax.ShapeDtypeStruct((1, LANES), F32), ja...  34.7 us
    pallas_call x1, Pallas kernels, shards(): pl.pallas_call(publish, out_shape=[jax.ShapeDtypeStruct(result.shape, res...  0.82 us

profile of v8, /device:TPU:0, one launch (start us, length us, event | category | flops | bytes accessed | tf_op | source)
XLA Modules:
  0.0 36.2 jit_solution(6828108885396091446)
XLA Ops:
  0.6 34.7 %shard_map.94 = (f32[1,128]{1,0:T(1,128)S(1)}, f32[128,512]{1,0:T(8,128)S(1)}, f32[128,512]{1,0:T(8,128)S(1)}) custom-call(bf16[128,512]{1,0:T(8,128)(2,1)} %pb_hbm.1, bf16[128,512]{1,0:T(8,128)(2,1)} %w_hbm.1, bf16[1,128]{1,0:T(2,128)(2,1)} %bitcast.9, s32[16,128]{1,0:T(8,128)} %bitcast.6, s32[4,128]{1,0:T(4,128)} %bitcast.7, f32[16]{0:T(128)} %level_hbm.1, ...), custom_call_target="tpu_custom_call" | custom-call | tf_op jit(solution)/shard_map/pallas_call | solution.py:1077
  35.4 0.8 %shard_map.95 = (f32[1,128]{1,0:T(1,128)}, f32[128,512]{1,0:T(8,128)}, f32[128,512]{1,0:T(8,128)}) custom-call(f32[1,128]{1,0:T(1,128)S(1)} %get-tuple-element.9.refs_0_, f32[128,512]{1,0:T(8,128)S(1)} %get-tuple-element.10.refs_1_, f32[128,512]{1,0:T(8,128)S(1)} %get-tuple-element.11.refs_2_), custom_call_target="tpu_custom_call" | custom-call | tf_op jit(solution)/shard_map/pallas_call | solution.py:1112
